TPU v7x, 256 devices: a whole 4x4x8 slice. The times are simulated.
256 devices in a mesh: ctx: 32 (over x_lo, z, core), tp: 8 (over x_hi, y).
Axes of the slice: x: 4 (x_hi: 2, x_lo: 2; x = x_hi * 2 + x_lo), y: 4, z: 8, core: 2. Of those that a mesh axis runs over, the one named last changes fastest.
Arguments:
- patches: bfloat16 [4, 4096, 6144], P(None, 'ctx', 'tp'), may hold values from -24 to 24
- ln_gain: float32 [6144], replicated, may hold values from 0.25 to 1.75
- w_qkv: bfloat16 [6144, 3, 24, 128], P('ctx', None, 'tp'), may hold values from -0.078125 to 0.078125
- query_gain: float32 [24, 128], P('tp'), may hold values from 0.5 to 8
- key_gain: float32 [24, 128], P('tp'), may hold values from 0.5 to 8
Outputs:
- attended: bfloat16 [4, 4096, 24, 128], P(None, 'ctx', 'tp')
All inputs are finite; a program needn't handle non-finite values.
Results may differ from a plain program's by a relative error of at most 0.007.
The roundings to bfloat16 on the way count: a program that leaves them out, or rounds other values in their place, can miss the bound.
Values may be sent and summed in bfloat16 or wider, within the bound.
No kernel may reach another device: no remote copies, remote signals or barrier semaphores. Data moves between devices by JAX's collectives and lax.ppermute only.
A program may use at most 192 MiB of HBM per device.

v0:
```python
import jax
import jax.numpy as jnp
from jax import lax
from jax.sharding import PartitionSpec as P

D = 6144


def layer_norm(values_in, gain):
    center = jnp.mean(values_in, axis=-1, keepdims=True)
    spread = jnp.mean(values_in * values_in, axis=-1, keepdims=True) - center * center
    return (values_in - center) * lax.rsqrt(spread + 1e-06) * gain


def shards(patches, ln_gain, w_qkv, query_gain, key_gain):
    crops, positions, local_width = patches.shape
    local_heads = w_qkv.shape[2]
    head_size = w_qkv.shape[3]
    score_scale = 1.0 / jnp.sqrt(jnp.float32(head_size))
    gathered = lax.all_gather(patches, "tp", axis=2, tiled=True)
    normed = layer_norm(gathered.astype(jnp.float32), ln_gain).astype(jnp.bfloat16)
    normed_rows = normed.reshape(crops * positions, D)

    def add_panel(panel):
        return jnp.dot(
            normed_rows, panel.reshape(panel.shape[0], -1), preferred_element_type=jnp.float32
        )

    query_raw = add_panel(lax.all_gather(w_qkv[:, 0], "ctx", axis=0, tiled=True))
    key_raw = add_panel(lax.all_gather(w_qkv[:, 1], "ctx", axis=0, tiled=True))
    value_raw = add_panel(lax.all_gather(w_qkv[:, 2], "ctx", axis=0, tiled=True))
    query_raw = query_raw.reshape(crops, positions, local_heads, head_size)
    key_raw = key_raw.reshape(crops, positions, local_heads, head_size)
    value_raw = value_raw.reshape(crops, positions, local_heads, head_size)
    queries = layer_norm(query_raw, query_gain).astype(jnp.bfloat16)
    keys_local = layer_norm(key_raw, key_gain).astype(jnp.bfloat16)
    values_local = value_raw.astype(jnp.bfloat16)
    best = jnp.full((crops, local_heads, positions), -jnp.inf, jnp.float32)
    totals = jnp.zeros((crops, local_heads, positions), jnp.float32)
    accum = jnp.zeros((crops, local_heads, positions, head_size), jnp.float32)
    key_block = lax.all_gather(keys_local, "ctx", axis=1, tiled=True)
    value_block = lax.all_gather(values_local, "ctx", axis=1, tiled=True)
    scores = (
        jnp.einsum("cqhd,ckhd->chqk", queries, key_block, preferred_element_type=jnp.float32)
        * score_scale
    )
    new_best = jnp.max(scores, axis=-1)
    correction = jnp.exp(best - new_best)
    expd = jnp.exp(scores - new_best[..., None])
    totals = totals * correction + jnp.sum(expd, axis=-1)
    probs = expd.astype(jnp.bfloat16)
    accum = accum * correction[..., None] + jnp.einsum(
        "chqk,ckhd->chqd", probs, value_block, preferred_element_type=jnp.float32
    )
    best, totals, accum = (new_best, totals, accum)
    result = accum / totals[..., None]
    return jnp.transpose(result, (0, 2, 1, 3)).astype(jnp.bfloat16)


def solution(mesh):
    return jax.shard_map(
        shards,
        mesh=mesh,
        in_specs=(
            P(None, "ctx", "tp"),
            P(),
            P("ctx", None, "tp", None),
            P("tp", None),
            P("tp", None),
        ),
        out_specs=P(None, "ctx", "tp", None),
        check_vma=False,
    )
```

profile of v0, /device:TPU:1, one launch (start us, length us, event | category | flops | bytes accessed | tf_op | source)
XLA Modules:
  0.0 524.1 jit_solution(13115239503239996337)
XLA Ops:
  6.5 0.0 copy-start.2
  6.5 0.0 all-gather.18.cloned.1.call-start
  6.5 1.8 fusion.42
  8.4 0.0 all-gather.18.cloned.1.call-update
  8.4 0.0 all-gather.10.cloned.1.call-start
  8.4 0.7 all-gather.10.cloned.1.call-update
  9.1 0.0 all-gather.20.cloned.1.call-start
  9.2 0.7 all-gather.20.cloned.1.call-update
  9.9 0.0 all-gather.16.cloned.1.call-start
  9.9 0.5 all-gather.16.cloned.1.call-update
  10.4 0.0 all-gather.12.cloned.1.call-start
  10.5 70.7 %all-gather.18.cloned.1.call-done = bf16[6144,1,3,128]{3,0,2,1:T(8,128)(2,1)} async-done(((bf16[192,1,3,128]{3,0,2,1:T(8,128)(2,1)}), bf16[6144,1,3,128]{3,0,2,1:T(8,128)(2,1)}) %all-gather.18.cloned.1.call-update) | async-done | bytes 4718608 | tf_op jit(solution)/shard_map/all_gather | solution.py:30
  81.2 6.7 %copy.14 = bf16[6144,1,3,128]{0,3,2,1:T(8,128)(2,1)} copy(bf16[6144,1,3,128]{3,0,2,1:T(8,128)(2,1)} %all-gather.18.cloned.1.call-done) | data formatting | bytes 9437184 | tf_op jit(solution)/shard_map/all_gather | solution.py:30
  87.9 88.3 %all-gather.10.cloned.1.call-done = bf16[4,128,6144]{2,1,0:T(8,128)(2,1)} async-done(((bf16[4,128,768]{2,1,0:T(8,128)(2,1)}), bf16[4,128,6144]{2,1,0:T(8,128)(2,1)}) %all-gather.10.cloned.1.call-update) | async-done | bytes 6291472 | tf_op jit(solution)/shard_map/all_gather | solution.py:20
  176.2 4.8 convert_reduce_fusion
  181.0 0.0 copy-done.2
  181.0 0.0 copy-start.1
  181.0 6.6 %fusion.41 = (f32[4,128,3]{1,2,0:T(4,128)S(1)}, f32[4,128,3]{1,2,0:T(4,128)S(1)}, f32[4,128,3,128]{1,3,2,0:T(8,128)S(1)}) fusion(bf16[6144,1,3,128]{0,3,2,1:T(8,128)(2,1)} %copy.14, bf16[4,128,6144]{2,1,0:T(8,128)(2,1)} %all-gather.10.cloned.1.call-done, f32[6144]{0:T(1024)S(1)} %copy-done.2, f32[4,128]{1,0:T(4,128)S(1)} %get-tuple-element.19, ...), kind=kOutput, calls=%fused_computation.44 | convolution fusion | flops 2432234496 | bytes 11837440 | tf_op jit(solution)/shard_map/dot_general | solution.py:25
  187.7 0.0 copy-done.1
  187.7 0.9 multiply_convert_fusion
  188.6 0.0 all-gather.12.cloned.1.call-update
  188.6 0.2 all-gather.14.cloned.1.call-start
  188.8 55.3 %all-gather.20.cloned.1.call-done = bf16[6144,1,3,128]{3,0,2,1:T(8,128)(2,1)} async-done(((bf16[192,1,3,128]{3,0,2,1:T(8,128)(2,1)}), bf16[6144,1,3,128]{3,0,2,1:T(8,128)(2,1)}) %all-gather.20.cloned.1.call-update) | async-done | bytes 4718608 | tf_op jit(solution)/shard_map/all_gather | solution.py:31
  244.2 6.7 %copy.17 = bf16[6144,1,3,128]{0,3,2,1:T(8,128)(2,1)} copy(bf16[6144,1,3,128]{3,0,2,1:T(8,128)(2,1)} %all-gather.20.cloned.1.call-done) | data formatting | bytes 9437184 | tf_op jit(solution)/shard_map/all_gather | solution.py:31
  250.8 7.7 %fusion.23 = bf16[4,128,3,128]{3,1,2,0:T(8,128)(2,1)} fusion(bf16[6144,1,3,128]{0,3,2,1:T(8,128)(2,1)} %copy.17, bf16[4,128,6144]{2,1,0:T(8,128)(2,1)} %all-gather.10.cloned.1.call-done, f32[6144]{0:T(1024)S(1)} %copy-done.2, f32[4,128]{1,0:T(4,128)S(1)} %get-tuple-element.19, f32[4,128]{1,0:T(4,128)S(1)} %get-tuple-element.18), kind=kOutput, calls=%fused_computation.23 | convolution fusion | flops 2431844352 | bytes 11431936 | tf_op jit(solution)/shard_map/dot_general | solution.py:25
  258.5 0.0 all-gather.14.cloned.1.call-update
  258.6 55.2 %all-gather.16.cloned.1.call-done = bf16[6144,1,3,128]{3,0,2,1:T(8,128)(2,1)} async-done(((bf16[192,1,3,128]{3,0,2,1:T(8,128)(2,1)}), bf16[6144,1,3,128]{3,0,2,1:T(8,128)(2,1)}) %all-gather.16.cloned.1.call-update) | async-done | bytes 4718608 | tf_op jit(solution)/shard_map/all_gather | solution.py:29
  313.8 6.7 %copy.13 = bf16[6144,1,3,128]{0,3,2,1:T(8,128)(2,1)} copy(bf16[6144,1,3,128]{3,0,2,1:T(8,128)(2,1)} %all-gather.16.cloned.1.call-done) | data formatting | bytes 9437184 | tf_op jit(solution)/shard_map/all_gather | solution.py:29
  320.5 0.0 copy-start
  320.5 6.6 %fusion.40 = (f32[4,128,3]{1,2,0:T(4,128)S(1)}, f32[4,128,3]{1,2,0:T(4,128)S(1)}, f32[4,128,3,128]{1,3,2,0:T(8,128)S(1)}) fusion(bf16[6144,1,3,128]{0,3,2,1:T(8,128)(2,1)} %copy.13, bf16[4,128,6144]{2,1,0:T(8,128)(2,1)} %all-gather.10.cloned.1.call-done, f32[6144]{0:T(1024)S(1)} %copy-done.2, f32[4,128]{1,0:T(4,128)S(1)} %get-tuple-element.19, ...), kind=kOutput, calls=%fused_computation.43 | convolution fusion | flops 2432234496 | bytes 11837440 | tf_op jit(solution)/shard_map/dot_general | solution.py:25
  327.1 95.4 %all-gather.12.cloned.1.call-done = bf16[4,4096,3,128]{1,3,2,0:T(8,128)(2,1)} async-done(((bf16[4,128,3,128]{1,3,2,0:T(8,128)(2,1)}), bf16[4,4096,3,128]{1,3,2,0:T(8,128)(2,1)}) %all-gather.12.cloned.1.call-update) | async-done | bytes 12582928 | tf_op jit(solution)/shard_map/all_gather | solution.py:41
  422.5 0.0 copy-done
  422.5 17.0 %multiply_reduce_fusion = (f32[4,3,128]{2,1,0:T(4,128)S(1)}, f32[4,3,128,4096]{3,2,1,0:T(8,128)}) fusion(bf16[4,4096,3,128]{1,3,2,0:T(8,128)(2,1)} %all-gather.12.cloned.1.call-done, f32[4,128,3,128]{1,3,2,0:T(8,128)S(1)} %get-tuple-element.21, f32[3,128]{1,0:T(4,128)S(1)} %copy-done, f32[4,128,3]{1,2,0:T(4,128)S(1)} %get-tuple-element.15, ...), kind=kOutput, calls=%fused_computation.1 | convolution fusion | flops 1623980544 | bytes 38555136 | tf_op jit(solution)/shard_map/cqhd,ckhd->chqk/dot_general | solution.py:44
  439.4 11.2 %fusion = f32[4,3,128]{2,1,0:T(4,128)S(1)} fusion(f32[4,3,128,4096]{3,2,1,0:T(8,128)} %get-tuple-element.23, f32[4,3,128]{2,1,0:T(4,128)S(1)} %get-tuple-element.22), kind=kLoop, calls=%fused_computation.2 | loop fusion | flops 18872832 | bytes 25178112 | tf_op jit(solution)/shard_map/reduce_sum | solution.py:50
  450.6 51.4 %all-gather.14.cloned.1.call-done = bf16[4,4096,3,128]{3,1,2,0:T(8,128)(2,1)} async-done(((bf16[4,128,3,128]{3,1,2,0:T(8,128)(2,1)}), bf16[4,4096,3,128]{3,1,2,0:T(8,128)(2,1)}) %all-gather.14.cloned.1.call-update) | async-done | bytes 12582928 | tf_op jit(solution)/shard_map/all_gather | solution.py:42
  502.0 15.3 %fusion.29 = bf16[4,128,3,128]{3,1,2,0:T(8,128)(2,1)} fusion(bf16[4,4096,3,128]{3,1,2,0:T(8,128)(2,1)} %all-gather.14.cloned.1.call-done, f32[4,3,128,4096]{3,2,1,0:T(8,128)} %get-tuple-element.23, f32[4,3,128]{2,1,0:T(4,128)S(1)} %get-tuple-element.22, f32[4,128,3]{1,2,0:T(4,128)S(1)} %bitcast_add_fusion, f32[4,128,3]{1,2,0:T(4,128)S(1)} %multiply_bitcast_fusion), kind=kOutput, calls=%fused_computation.25 | convolution fusion | flops 1630076928 | bytes 38160384 | tf_op jit(solution)/shard_map/chqk,ckhd->chqd/dot_general | solution.py:52
  (5 shorter events, 0.1 us)
Async XLA Ops:
  6.5 174.5 %copy-start.2 = (f32[6144]{0:T(1024)S(1)}, f32[6144]{0:T(1024)}, u32[]{:S(2)}) copy-start(f32[6144]{0:T(1024)} %param.6) | copy-start | bytes 73732
  6.5 74.7 %all-gather.18.cloned.1.call-start = ((), (), s32[]{:S(2)}) async-start(), calls=%async_computation.4 | async-start | bytes 4866048 | tf_op jit(solution)/shard_map/all_gather | solution.py:30
  8.4 167.8 %all-gather.10.cloned.1.call-start = ((), (), s32[]{:S(2)}) async-start(), calls=%async_computation | async-start | bytes 7077888 | tf_op jit(solution)/shard_map/all_gather | solution.py:20
  9.1 235.0 %all-gather.20.cloned.1.call-start = ((), (), s32[]{:S(2)}) async-start(), calls=%async_computation.5 | async-start | bytes 4866048 | tf_op jit(solution)/shard_map/all_gather | solution.py:31
  9.9 303.9 %all-gather.16.cloned.1.call-start = ((), (), s32[]{:S(2)}) async-start(), calls=%async_computation.3 | async-start | bytes 4866048 | tf_op jit(solution)/shard_map/all_gather | solution.py:29
  10.4 412.0 %all-gather.12.cloned.1.call-start = ((), (), s32[]{:S(2)}) async-start(), calls=%async_computation.1 | async-start | bytes 12976128 | tf_op jit(solution)/shard_map/all_gather | solution.py:41
  181.0 6.6 %copy-start.1 = (f32[3,128]{1,0:T(4,128)S(1)}, f32[3,128]{1,0:T(4,128)}, u32[]{:S(2)}) copy-start(f32[3,128]{1,0:T(4,128)} %param.9) | copy-start | bytes 4612
  188.6 313.4 %all-gather.14.cloned.1.call-start = ((), (), s32[]{:S(2)}) async-start(), calls=%async_computation.2 | async-start | bytes 12976128 | tf_op jit(solution)/shard_map/all_gather | solution.py:42
  320.5 102.0 %copy-start = (f32[3,128]{1,0:T(4,128)S(1)}, f32[3,128]{1,0:T(4,128)}, u32[]{:S(2)}) copy-start(f32[3,128]{1,0:T(4,128)} %param.8) | copy-start | bytes 4612
Sparse Core Ops, SparseCore 0:
  9.2 72.0 all-gather.17
  83.8 92.3 all-gather.9
  178.0 66.1 all-gather.19
  245.8 67.8 all-gather.15
  315.4 107.0 all-gather.11
  424.2 77.7 all-gather.13
where the time goes:
time: 525 us; the launch traced here: 524 us
  waiting for transfers between devices  418 us (80%)
  matrix products  53.1 us (10%)
  local copies, waits for them, and re-layouts  21.8 us (4%)
  other arithmetic  17 us (3%)
  between operations  13.5 us (3%)
    all_gather x1, waiting for transfers between devices, shards(): key_block = lax.all_gather(keys_local, 'ctx', axis=1, tiled=True)  95.4 us
    all_gather x1, waiting for transfers between devices, shards(): gathered = lax.all_gather(patches, 'tp', axis=2, tiled=True)  88.3 us
    all_gather x1, waiting for transfers between devices, shards(): key_raw = add_panel(lax.all_gather(w_qkv[:, 1], 'ctx', axis=0, tiled=True))  70.7 us
    all_gather x1, waiting for transfers between devices, shards(): lax.all_gather(w_qkv[:, 2], 'ctx', axis=0, tiled=True)  55.3 us
    all_gather x1, waiting for transfers between devices, shards(): lax.all_gather(w_qkv[:, 0], 'ctx', axis=0, tiled=True)  55.2 us
    all_gather x1, waiting for transfers between devices, shards(): value_block = lax.all_gather(values_local, 'ctx', axis=1, tiled=True)  51.4 us
    dot_general x3, matrix products, add_panel(): jnp.dot(normed_rows, panel.reshape(panel.shape[0], -1), preferred_element...  20.9 us
    dot_general x1, matrix products, shards(): jnp.einsum('cqhd,ckhd->chqk', queries, key_block, preferred_element_type=...  17 us
  transfers between devices with their start and end apart: 6, of which 6 were waited for; matrix products, arithmetic and copies ran while one was open for 14% of the time, Pallas kernels for 0%

commit v1 on v0

v1 whole, which is shorter than its diff:
```python
import jax
import jax.numpy as jnp
from jax import lax
from jax.experimental import pallas as pl
from jax.experimental.pallas import tpu as pltpu
from jax.sharding import Mesh, PartitionSpec as P

TP = 8
KB = 768
SUB = 192
HD = 128
SWAP = [(0, 1), (1, 0)]
VMEM_LIMIT = 58 * 1024 * 1024
ANY = pl.BlockSpec(memory_space=pl.ANY)


def ring(n, shift):
    return [(i, (i + shift) % n) for i in range(n)]


def features_index(xh, y, a, b):
    return lax.rem(xh + a, 2) * 4 + lax.rem(y + b, 4)


def norm_kernel(*refs):
    pieces, gain_ref, out_ref, held, sems = refs[:12], refs[12], refs[13], refs[14], refs[15]
    xh, y = lax.axis_index("xh"), lax.axis_index("y")
    row0 = 0
    copies = []
    for chunk in range(2):
        c0, c1, f, b, g, h = pieces[6 * chunk : 6 * chunk + 6]
        rows = c0.shape[0]
        plan = (
            (c0, 0, 0),
            (c1, 1, 0),
            (f.at[0], 0, 3),
            (f.at[1], 1, 3),
            (b.at[0], 0, 1),
            (b.at[1], 1, 1),
            (g, 0, 2),
            (h, 1, 2),
        )
        for src, dx, dy in plan:
            t = features_index(xh, y, dx, dy)
            copy = pltpu.make_async_copy(
                src, held.at[t, pl.ds(row0, rows), :], sems.at[len(copies)]
            )
            copy.start()
            copies.append(copy)
        row0 += rows
    tile = 16

    def rows_step(i, carry):
        r = pl.multiple_of(i * tile, tile)
        total = jnp.zeros((tile, 1), jnp.float32)
        square = jnp.zeros((tile, 1), jnp.float32)
        part = jnp.zeros((tile, 128), jnp.float32)
        part2 = jnp.zeros((tile, 128), jnp.float32)
        for t in range(TP):
            block = held[t, pl.ds(r, tile), :].astype(jnp.float32)
            for j in range(KB // 128):
                piece = block[:, j * 128 : (j + 1) * 128]
                part = part + piece
                part2 = part2 + piece * piece
        total = jnp.sum(part, axis=-1, keepdims=True)
        square = jnp.sum(part2, axis=-1, keepdims=True)
        center = total * (1.0 / (TP * KB))
        spread = square * (1.0 / (TP * KB)) - center * center
        scale = lax.rsqrt(spread + 1e-06)
        for t in range(TP):
            block = held[t, pl.ds(r, tile), :].astype(jnp.float32)
            out_ref[t, pl.ds(r, tile), :] = (
                (block - center) * scale * gain_ref[t : t + 1, :]
            ).astype(jnp.bfloat16)
        return carry

    split = pieces[0].shape[0] // tile
    for copy in copies[:8]:
        copy.wait()
    lax.fori_loop(0, split, rows_step, 0)
    for copy in copies[8:]:
        copy.wait()
    lax.fori_loop(split, row0 // tile, rows_step, 0)


def norm_rows(pieces, gain):
    return pl.pallas_call(
        norm_kernel,
        out_shape=jax.ShapeDtypeStruct((TP, 512, KB), jnp.bfloat16),
        in_specs=[ANY] * 12 + [pl.BlockSpec(memory_space=pltpu.VMEM)],
        out_specs=pl.BlockSpec(memory_space=pltpu.VMEM),
        scratch_shapes=[
            pltpu.VMEM((TP, 512, KB), jnp.bfloat16),
            pltpu.SemaphoreType.DMA((16,)),
        ],
        compiler_params=pltpu.CompilerParams(vmem_limit_bytes=VMEM_LIMIT),
    )(*pieces, gain)


def head_norm(values_in, gain):
    center = jnp.mean(values_in, axis=-1, keepdims=True)
    spread = jnp.mean(values_in * values_in, axis=-1, keepdims=True) - center * center
    return (values_in - center) * lax.rsqrt(spread + 1e-06) * gain


def load_weight(parts, held, col, sems, first):
    xl, core = lax.axis_index("xl"), lax.axis_index("core")
    copies = []
    for dc, dx, piece in parts:
        for z in range(8):
            t = lax.rem(xl + dx, 2) * 4 + z // 2
            copies.append(
                pltpu.make_async_copy(
                    piece.at[z],
                    held.at[t, z % 2, lax.rem(core + dc, 2), :, pl.ds(col, 384)],
                    sems.at[first + len(copies)],
                )
            )
    return copies


def project_kv_kernel(x_ref, *refs):
    k_parts, v_parts, gain_ref, kv_ref, held, total, sems = (
        refs[:4], refs[4:6], refs[6], refs[7], refs[8], refs[9], refs[10]
    )
    own = [(0, 0, k_parts[0]), (0, 1, k_parts[1]), (1, 0, k_parts[2]), (1, 1, k_parts[3])]
    copies = load_weight(own, held, 0, sems, 0)
    both = [(dc, dx, v_parts[dc].at[dx]) for dc in range(2) for dx in range(2)]
    copies += load_weight(both, held, 384, sems, 32)
    for copy in copies:
        copy.start()
    for copy in copies:
        copy.wait()
    total[...] = jnp.zeros_like(total)

    def step(t, carry):
        weight = held[t].reshape(KB, 768)
        total[...] += jnp.dot(x_ref[t], weight, preferred_element_type=jnp.float32)
        return carry

    lax.fori_loop(0, TP, step, 0)
    for h in range(3):
        cols = slice(h * HD, (h + 1) * HD)
        kv_ref[:, cols] = head_norm(total[:, cols], gain_ref[h : h + 1, :]).astype(jnp.bfloat16)
    kv_ref[:, 384:] = total[:, 384:].astype(jnp.bfloat16)


def project_q_kernel(x_ref, *refs):
    q_parts, gain_ref, q_ref, held, total, sems = refs[:2], refs[2], refs[3], refs[4], refs[5], refs[6]
    both = [(dc, dx, q_parts[dc].at[dx]) for dc in range(2) for dx in range(2)]
    copies = load_weight(both, held, 0, sems, 0)
    for copy in copies:
        copy.start()
    for copy in copies:
        copy.wait()
    total[...] = jnp.zeros_like(total)

    def step(t, carry):
        weight = held[t].reshape(KB, 384)
        total[...] += jnp.dot(x_ref[t], weight, preferred_element_type=jnp.float32)
        return carry

    lax.fori_loop(0, TP, step, 0)
    for h in range(3):
        cols = slice(h * HD, (h + 1) * HD)
        q_ref[:, cols] = head_norm(total[:, cols], gain_ref[h : h + 1, :]).astype(jnp.bfloat16)


VM = pl.BlockSpec(memory_space=pltpu.VMEM)


def project(kernel, normed, parts, gain, width):
    n = len(parts)
    return pl.pallas_call(
        kernel,
        out_shape=jax.ShapeDtypeStruct((512, width), jnp.bfloat16),
        in_specs=[VM] + [ANY] * n + [VM],
        out_specs=VM,
        scratch_shapes=[
            pltpu.VMEM((TP, 2, 2, SUB, width), jnp.bfloat16),
            pltpu.VMEM((512, width), jnp.float32),
            pltpu.SemaphoreType.DMA((32 * (width // 384),)),
        ],
        compiler_params=pltpu.CompilerParams(vmem_limit_bytes=VMEM_LIMIT),
    )(normed, *parts, gain)


def attend_kernel(n_parts, q_ref, *refs):
    parts, outs, held, sems = refs[:n_parts], refs[n_parts : n_parts + 4], refs[-2], refs[-1]
    row = 0
    copies = []
    for i, part in enumerate(parts):
        rows = part.shape[0]
        copies.append(pltpu.make_async_copy(part, held.at[pl.ds(row, rows), :], sems.at[i]))
        row += rows
    for copy in copies:
        copy.start()
    for copy in copies:
        copy.wait()
    scale = 1.0 / (HD ** 0.5)
    for h in range(3):
        for s in range(4):
            q = q_ref[s * 128 : (s + 1) * 128, h * HD : (h + 1) * HD]
            keys = held[:, h * HD : (h + 1) * HD]
            scores = lax.dot_general(
                q, keys, (((1,), (1,)), ((), ())), preferred_element_type=jnp.float32
            ) * scale
            expd = jnp.exp(scores - jnp.max(scores, axis=-1, keepdims=True))
            totals = jnp.sum(expd, axis=-1, keepdims=True)
            values = held[:, 384 + h * HD : 384 + (h + 1) * HD]
            summed = jnp.dot(expd.astype(jnp.bfloat16), values, preferred_element_type=jnp.float32)
            outs[s][:, h * HD : (h + 1) * HD] = (summed / totals).astype(jnp.bfloat16)


def attend(queries, parts):
    n = len(parts)
    return pl.pallas_call(
        lambda *refs: attend_kernel(n, *refs),
        out_shape=[jax.ShapeDtypeStruct((128, 384), jnp.bfloat16)] * 4,
        in_specs=[VM] + [ANY] * n,
        out_specs=[VM] * 4,
        scratch_shapes=[
            pltpu.VMEM((4096, 768), jnp.bfloat16),
            pltpu.SemaphoreType.DMA((n,)),
        ],
        compiler_params=pltpu.CompilerParams(vmem_limit_bytes=VMEM_LIMIT),
    )(queries, *parts)


def shards(patches, ln_gain, w_qkv, query_gain, key_gain):
    zh = lax.axis_index("zh")

    def crop(s):
        return lax.dynamic_index_in_dim(patches, lax.rem(zh + s, 4), 0, keepdims=False)

    def weight(i):
        return w_qkv[:, i].reshape(SUB, 384)

    sent = [lax.ppermute(crop(s), "zh", ring(4, s)) for s in (1, 3, 2)]
    chunks = (crop(0), jnp.concatenate([sent[0], sent[2], sent[1]], axis=0))
    pieces = []
    for chunk in chunks:
        other = lax.ppermute(chunk, "xh", SWAP)
        pair = jnp.stack([chunk, other])
        fwd = lax.ppermute(pair, "y", ring(4, 1))
        bwd = lax.ppermute(pair, "y", ring(4, -1))
        far0 = lax.ppermute(fwd[0], "y", ring(4, 1))
        far1 = lax.ppermute(bwd[1], "y", ring(4, -1))
        pieces += [chunk, other, fwd, bwd, far0, far1]
    wk0 = lax.all_gather(weight(1), ("zh", "zl"), axis=0)
    wk1 = lax.ppermute(wk0, "xl", SWAP)
    wk2 = lax.ppermute(wk0, "core", SWAP)
    wk3 = lax.ppermute(wk1, "core", SWAP)

    def gather_pair(part):
        pair = jnp.stack([part, lax.ppermute(part, "xl", SWAP)])
        own = lax.all_gather(pair, ("zh", "zl"), axis=1)
        return own, lax.ppermute(own, "core", SWAP)

    wv = gather_pair(weight(2))
    wq = gather_pair(weight(0))

    normed = norm_rows(pieces, ln_gain.reshape(TP, KB))
    kv = project(project_kv_kernel, normed, (wk0, wk1, wk2, wk3) + wv, key_gain, 768)
    across_x = lax.ppermute(kv, "xl", SWAP)
    across_z = lax.ppermute(kv, "zl", SWAP)
    queries = project(project_q_kernel, normed, wq, query_gain, 384)
    diag0 = lax.ppermute(across_x[:256], "zl", SWAP)
    diag1 = lax.ppermute(across_z[256:], "xl", SWAP)
    mine = [kv, across_x, across_z, diag0, diag1]
    theirs = [lax.ppermute(part, "core", SWAP) for part in mine]
    outs = attend(queries, mine + theirs)
    back = [outs[0]] + [lax.ppermute(outs[s], "zh", ring(4, -s)) for s in (1, 2, 3)]
    doubled = jnp.stack(back + back)
    ordered = lax.dynamic_slice_in_dim(doubled, 4 - zh, 4, axis=0)
    return ordered.reshape(4, 128, 3, HD)


def solution(mesh):
    fine = Mesh(mesh.devices.reshape(2, 4, 2, 2, 2, 4), ("xl", "zh", "zl", "core", "xh", "y"))
    ctx, tp = ("xl", "zh", "zl", "core"), ("xh", "y")
    return jax.shard_map(
        shards,
        mesh=fine,
        in_specs=(P(None, ctx, tp), P(), P(ctx, None, tp, None), P(tp, None), P(tp, None)),
        out_specs=P(None, ctx, tp, None),
        check_vma=False,
    )
```

time: 525 us -> 315 us (0.60)
  waiting for transfers between devices: 418 us -> 155 us
  Pallas kernels: 0 us -> 63.9 us
  starting transfers between devices: 0.38 us -> 60.7 us
  matrix products: 53.1 us -> 0 us
  other arithmetic: 17 us -> 3.58 us
  local copies, waits for them, and re-layouts: 21.8 us -> 12.9 us
    all_gather x6 -> x3, waiting for transfers between devices: 416 us -> 45.7 us  [the longest x2 45.7 us: gather_pair(): own = lax.all_gather(pair, ('zh', 'zl'), axis=1)]
    ppermute x0 -> x32, waiting for transfers between devices: none -> 109 us  [the longest x2 20.3 us: shards(): far0 = lax.ppermute(fwd[0], 'y', ring(4, 1))]
    pallas_call x0 -> x4, Pallas kernels: none -> 63.9 us  [the longest x2 36.5 us: project(): pl.pallas_call(kernel, out_shape=jax.ShapeDtypeStruct((512, width), jnp.b...]
    ppermute x0 -> x32, starting transfers between devices: none -> 60.6 us  [the longest x5 11.2 us: shards(): theirs = [lax.ppermute(part, 'core', SWAP) for part in mine]]
    dot_general x5 -> x0, matrix products: 53.1 us -> none  [the longest x3 20.9 us: add_panel(): jnp.dot(normed_rows, panel.reshape(panel.shape[0], -1), preferred_element...]
    all_gather x3 -> x0, local copies, waits for them, and re-layouts: 20 us -> none  [the longest x1 6.68 us: shards(): lax.all_gather(w_qkv[:, 0], 'ctx', axis=0, tiled=True)]
    reduce_sum x2 -> x0, other arithmetic: 16 us -> none  [the longest x1 11.2 us: shards(): totals = totals * correction + jnp.sum(expd, axis=-1)]
  transfers between devices with their start and end apart: 6 -> 35, of which waited for: 6 -> 18; matrix products, arithmetic and copies ran while one was open for 14% -> 3% of each run, Pallas kernels for 0% -> 16%
where the time goes in v1:
time: 315 us; the launch traced here: 310 us
  waiting for transfers between devices  155 us (49%)
  Pallas kernels  63.9 us (20%)
  starting transfers between devices  60.7 us (19%)
  between operations  13.7 us (4%)
  local copies, waits for them, and re-layouts  12.9 us (4%)
  other arithmetic  3.58 us (1%)
    all_gather x2, waiting for transfers between devices, gather_pair(): own = lax.all_gather(pair, ('zh', 'zl'), axis=1)  45.7 us
    pallas_call x2, Pallas kernels, project(): pl.pallas_call(kernel, out_shape=jax.ShapeDtypeStruct((512, width), jnp.b...  36.5 us
    ppermute x2, waiting for transfers between devices, shards(): far0 = lax.ppermute(fwd[0], 'y', ring(4, 1))  20.3 us
    ppermute x3, waiting for transfers between devices, shards(): sent = [lax.ppermute(crop(s), 'zh', ring(4, s)) for s in (1, 3, 2)]  18.5 us
    pallas_call x1, Pallas kernels, attend(): pl.pallas_call(lambda *refs: attend_kernel(n, *refs), out_shape=[jax.Shap...  15.8 us
    ppermute x2, waiting for transfers between devices, shards(): far1 = lax.ppermute(bwd[1], 'y', ring(4, -1))  15.5 us
    ppermute x2, waiting for transfers between devices, shards(): other = lax.ppermute(chunk, 'xh', SWAP)  14.5 us
    ppermute x1, waiting for transfers between devices, shards(): across_x = lax.ppermute(kv, 'xl', SWAP)  12.1 us
  transfers between devices with their start and end apart: 35, of which 18 were waited for; matrix products, arithmetic and copies ran while one was open for 3% of the time, Pallas kernels for 16%

profile of v1, /device:TPU:1, one launch (start us, length us, event | category | flops | bytes accessed | tf_op | source)
XLA Modules:
  0.0 309.7 jit_solution(6784313728770932819)
XLA Ops:
  6.5 1.1 fusion
  8.8 2.1 collective-permute-start.18
  11.0 2.4 collective-permute-done.18
  14.5 2.0 collective-permute-start.13
  16.6 2.4 collective-permute-done.13
  19.0 0.8 pad_maximum_fusion.2
  19.9 3.6 %collective-permute-start.5 = (bf16[128,768]{1,0:T(8,128)(2,1)S(1)}, bf16[128,768]{1,0:T(8,128)(2,1)S(1)}, u32[]{:S(2)}, u32[]{:S(2)}) collective-permute-start(bf16[128,768]{1,0:T(8,128)(2,1)S(1)} %get-tuple-element.14), channel_id=1, source_target_pairs={{0,32},{32,64},{64,96},{96,0},{1,33},{33,65},{65,97},{97,1},{2,34}... | collective-permute-start | bytes 589832 | tf_op jit(solution)/shard_map/ppermute | solution.py:239
  23.5 5.1 %collective-permute-start.6 = (bf16[128,768]{1,0:T(8,128)(2,1)S(1)}, bf16[128,768]{1,0:T(8,128)(2,1)S(1)}, u32[]{:S(2)}, u32[]{:S(2)}) collective-permute-start(bf16[128,768]{1,0:T(8,128)(2,1)S(1)} %get-tuple-element.16), channel_id=1, source_target_pairs={{0,64},{32,96},{64,0},{96,32},{1,65},{33,97},{65,1},{97,33},{2,66}... | collective-permute-start | bytes 589832 | tf_op jit(solution)/shard_map/ppermute | solution.py:239
  28.6 2.4 collective-permute-start.7
  31.0 2.2 collective-permute-done.5
  33.2 14.4 %collective-permute-done.6 = bf16[128,768]{1,0:T(8,128)(2,1)S(1)} collective-permute-done((bf16[128,768]{1,0:T(8,128)(2,1)S(1)}, bf16[128,768]{1,0:T(8,128)(2,1)S(1)}, u32[]{:S(2)}, u32[]{:S(2)}) %collective-permute-start.6) | collective-permute-done | bytes 196640 | tf_op jit(solution)/shard_map/ppermute | solution.py:239
  47.7 1.8 collective-permute-done.7
  49.6 2.9 collective-permute-start.8
  52.6 14.5 %collective-permute-done.refs_1_ = bf16[128,768]{1,0:T(8,128)(2,1)S(1)} collective-permute-done((bf16[128,768]{1,0:T(8,128)(2,1)S(1)}, bf16[128,768]{1,0:T(8,128)(2,1)S(1)}, u32[]{:S(2)}, u32[]{:S(2)}) %collective-permute-start) | collective-permute-done | bytes 196640 | tf_op jit(solution)/shard_map/ppermute | solution.py:243
  67.1 0.8 pad_maximum_fusion.1
  67.9 1.6 collective-permute-start.1
  69.5 1.2 pad_maximum_fusion
  70.7 0.9 collective-permute-start.9
  71.6 1.9 collective-permute-start.10
  73.5 1.2 collective-permute-start.15
  74.7 26.6 %all-gather.10.cloned.1.call-done = bf16[2,1536,384]{2,1,0:T(8,128)(2,1)} async-done(((bf16[2,192,384]{2,1,0:T(8,128)(2,1)}), bf16[2,1536,384]{2,1,0:T(8,128)(2,1)}) %all-gather.10.cloned.1.call-update) | async-done | bytes 2359312 | tf_op jit(solution)/shard_map/all_gather | solution.py:257
  101.3 3.6 %collective-permute-start.19 = (bf16[2,8,192,384]{3,2,1,0:T(8,128)(2,1)}, bf16[2,8,192,384]{3,2,1,0:T(8,128)(2,1)}, u32[]{:S(2)}, u32[]{:S(2)}) collective-permute-start(bf16[2,8,192,384]{3,2,1,0:T(8,128)(2,1)} %bitcast.54), channel_id=1, source_target_pairs={{0,8},{8,0},{1,9},{9,1},{2,10},{10,2},{3,11},{11,3},{4,12},{12,4},... | collective-permute-start | bytes 7077896 | tf_op jit(solution)/shard_map/ppermute | solution.py:258
  104.9 2.5 collective-permute-start.2
  107.5 0.9 slice_bitcast_fusion.3
  108.4 7.9 %collective-permute-done.2.refs_3_ = bf16[2,128,768]{2,1,0:T(8,128)(2,1)} collective-permute-done((bf16[2,128,768]{2,1,0:T(8,128)(2,1)}, bf16[2,128,768]{2,1,0:T(8,128)(2,1)}, u32[]{:S(2)}, u32[]{:S(2)}) %collective-permute-start.2) | collective-permute-done | bytes 393248 | tf_op jit(solution)/shard_map/ppermute | solution.py:246
  116.3 0.9 collective-permute-start.3
  117.3 7.1 %collective-permute-done.3.refs_4_ = bf16[128,768]{1,0:T(8,128)(2,1)} collective-permute-done((bf16[128,768]{1,0:T(8,128)(2,1)S(1)}, bf16[128,768]{1,0:T(8,128)(2,1)}, u32[]{:S(2)}, u32[]{:S(2)}) %collective-permute-start.3) | collective-permute-done | bytes 196640 | tf_op jit(solution)/shard_map/ppermute | solution.py:247
  124.3 19.1 %all-gather.8.cloned.1.call-done = bf16[2,1536,384]{2,1,0:T(8,128)(2,1)} async-done(((bf16[2,192,384]{2,1,0:T(8,128)(2,1)}), bf16[2,1536,384]{2,1,0:T(8,128)(2,1)}) %all-gather.8.cloned.1.call-update) | async-done | bytes 2359312 | tf_op jit(solution)/shard_map/all_gather | solution.py:257
  143.4 3.6 %collective-permute-start.14 = (bf16[2,8,192,384]{3,2,1,0:T(8,128)(2,1)}, bf16[2,8,192,384]{3,2,1,0:T(8,128)(2,1)}, u32[]{:S(2)}, u32[]{:S(2)}) collective-permute-start(bf16[2,8,192,384]{3,2,1,0:T(8,128)(2,1)} %bitcast.56), channel_id=1, source_target_pairs={{0,8},{8,0},{1,9},{9,1},{2,10},{10,2},{3,11},{11,3},{4,12},{12,4},... | collective-permute-start | bytes 7077896 | tf_op jit(solution)/shard_map/ppermute | solution.py:258
  147.0 0.9 slice_bitcast_fusion.2
  148.0 2.9 collective-permute-start.4
  150.9 4.3 %collective-permute-done.4.refs_5_ = bf16[128,768]{1,0:T(8,128)(2,1)} collective-permute-done((bf16[128,768]{1,0:T(8,128)(2,1)S(1)}, bf16[128,768]{1,0:T(8,128)(2,1)}, u32[]{:S(2)}, u32[]{:S(2)}) %collective-permute-start.4) | collective-permute-done | bytes 196640 | tf_op jit(solution)/shard_map/ppermute | solution.py:248
  155.2 1.0 collective-permute-start.11
  156.3 1.1 collective-permute-start.16
  157.5 0.9 slice_bitcast_fusion
  158.4 13.2 %collective-permute-done.11.refs_10_ = bf16[384,768]{1,0:T(8,128)(2,1)S(1)} collective-permute-done((bf16[384,768]{1,0:T(8,128)(2,1)S(1)}, bf16[384,768]{1,0:T(8,128)(2,1)S(1)}, u32[]{:S(2)}, u32[]{:S(2)}) %collective-permute-start.11) | collective-permute-done | bytes 589856 | tf_op jit(solution)/shard_map/ppermute | solution.py:247
  171.7 0.9 copy-done.12
  172.5 1.1 collective-permute-start.12
  173.7 1.3 reshape.6.refs_12_
  175.0 11.2 %collective-permute-done.12.refs_11_ = bf16[384,768]{1,0:T(8,128)(2,1)S(1)} collective-permute-done((bf16[384,768]{1,0:T(8,128)(2,1)}, bf16[384,768]{1,0:T(8,128)(2,1)S(1)}, u32[]{:S(2)}, u32[]{:S(2)}) %collective-permute-start.12) | collective-permute-done | bytes 589856 | tf_op jit(solution)/shard_map/ppermute | solution.py:248
  186.2 0.9 copy-done.13
  187.1 11.6 %shard_map.55.x_ref = bf16[8,512,768]{2,1,0:T(8,128)(2,1)} custom-call(bf16[128,768]{1,0:T(8,128)(2,1)} %bitcast.62, bf16[128,768]{1,0:T(8,128)(2,1)} %copy-done.11, bf16[2,128,768]{2,1,0:T(8,128)(2,1)} %collective-permute-done.1.refs_2_, bf16[2,128,768]{2,1,0:T(8,128)(2,1)} %collective-permute-done.2.refs_3_, ...), custom_call_target="tpu_custom_call" | custom-call | tf_op jit(solution)/shard_map/pallas_call | solution.py:87
  198.7 14.8 %shard_map.57.refs_1_ = bf16[512,768]{1,0:T(8,128)(2,1)} custom-call(bf16[8,512,768]{2,1,0:T(8,128)(2,1)} %shard_map.55.x_ref, bf16[8,192,384]{2,1,0:T(8,128)(2,1)} %all-gather.6.cloned.1.call-done.refs_0_, bf16[8,192,384]{2,1,0:T(8,128)(2,1)} %collective-permute-done.15.refs_1_, bf16[8,192,384]{2,1,0:T(8,128)(2,1)} %collective-permute-done.16.refs_2_, ...), custom_call_target="tpu_custom_call" | custom-call | tf_op jit(solution)/shard_map/pallas_call | solution.py:174
  213.6 1.2 collective-permute-start.20
  214.7 1.0 collective-permute-start.21
  215.7 2.8 collective-permute-start.24
  218.5 12.1 %collective-permute-done.20.refs_2_ = bf16[512,768]{1,0:T(8,128)(2,1)S(1)} collective-permute-done((bf16[512,768]{1,0:T(8,128)(2,1)}, bf16[512,768]{1,0:T(8,128)(2,1)S(1)}, u32[]{:S(2)}, u32[]{:S(2)}) %collective-permute-start.20) | collective-permute-done | bytes 786464 | tf_op jit(solution)/shard_map/ppermute | solution.py:265
  230.6 0.8 collective-permute-start.22
  231.5 3.5 %collective-permute-start.25 = (bf16[512,768]{1,0:T(8,128)(2,1)S(1)}, bf16[512,768]{1,0:T(8,128)(2,1)S(1)}, u32[]{:S(2)}, u32[]{:S(2)}) collective-permute-start(bf16[512,768]{1,0:T(8,128)(2,1)S(1)} %collective-permute-done.20.refs_2_), channel_id=1, source_target_pairs={{0,8},{8,0},{1,9},{9,1},{2,10},{10,2},{3,11},{11,3},{4,12},{12,4},... | collective-permute-start | bytes 2359304 | tf_op jit(solution)/shard_map/ppermute | solution.py:271
  235.0 1.0 collective-permute-start.26
  236.5 3.9 %collective-permute-done.22.refs_4_ = bf16[256,768]{1,0:T(8,128)(2,1)S(1)} collective-permute-done((bf16[256,768]{1,0:T(8,128)(2,1)S(1)}, bf16[256,768]{1,0:T(8,128)(2,1)S(1)}, u32[]{:S(2)}, u32[]{:S(2)}) %collective-permute-start.22) | collective-permute-done | bytes 393248 | tf_op jit(solution)/shard_map/ppermute | solution.py:268
  240.4 2.9 collective-permute-start.27
  243.3 3.5 %collective-permute-done.23.refs_5_ = bf16[256,768]{1,0:T(8,128)(2,1)} collective-permute-done((bf16[256,768]{1,0:T(8,128)(2,1)S(1)}, bf16[256,768]{1,0:T(8,128)(2,1)}, u32[]{:S(2)}, u32[]{:S(2)}) %collective-permute-start.23) | collective-permute-done | bytes 393248 | tf_op jit(solution)/shard_map/ppermute | solution.py:269
  246.8 0.9 collective-permute-start.28
  247.7 21.6 %shard_map.56.refs_0_ = bf16[512,384]{1,0:T(8,128)(2,1)} custom-call(bf16[8,512,768]{2,1,0:T(8,128)(2,1)} %shard_map.55.x_ref, bf16[2,8,192,384]{3,2,1,0:T(8,128)(2,1)} %bitcast.57, bf16[2,8,192,384]{3,2,1,0:T(8,128)(2,1)} %collective-permute-done.14.refs_1_, f32[3,128]{1,0:T(4,128)} %refs_2_.1), custom_call_target="tpu_custom_call" | custom-call | tf_op jit(solution)/shard_map/pallas_call | solution.py:174
  269.4 0.9 copy-done.8
  270.5 15.8 %shard_map.58 = (bf16[128,384]{1,0:T(8,128)(2,1)}, bf16[128,384]{1,0:T(8,128)(2,1)}, bf16[128,384]{1,0:T(8,128)(2,1)}, bf16[128,384]{1,0:T(8,128)(2,1)}) custom-call(bf16[512,384]{1,0:T(8,128)(2,1)} %shard_map.56.refs_0_, bf16[512,768]{1,0:T(8,128)(2,1)} %shard_map.57.refs_1_, bf16[512,768]{1,0:T(8,128)(2,1)} %copy-done.4, bf16[512,768]{1,0:T(8,128)(2,1)} %copy-done.5, ...), custom_call_target="tpu_custom_call" | custom-call | tf_op jit(solution)/shard_map/pallas_call | solution.py:217
  286.4 2.4 collective-permute-start.29
  288.8 0.9 bitcast_dynamic-update-slice_fusion.6
  289.7 2.8 collective-permute-start.30
  292.4 1.4 collective-permute-done.29
  293.8 6.9 %collective-permute-done.30 = bf16[128,384]{1,0:T(8,128)(2,1)S(1)} collective-permute-done((bf16[128,384]{1,0:T(8,128)(2,1)}, bf16[128,384]{1,0:T(8,128)(2,1)S(1)}, u32[]{:S(2)}, u32[]{:S(2)}) %collective-permute-start.30) | collective-permute-done | bytes 98336 | tf_op jit(solution)/shard_map/ppermute | solution.py:273
  300.8 0.9 bitcast_dynamic-update-slice_fusion.7
  302.1 0.9 copy.20
  (78 shorter events, 4.1 us)
Async XLA Ops:
  6.5 66.9 %all-gather.6.cloned.1.call-start = ((), (), s32[]{:S(2)}) async-start(), calls=%async_computation | async-start | bytes 1327104 | tf_op jit(solution)/shard_map/all_gather | solution.py:250
  8.6 92.7 %all-gather.10.cloned.1.call-start = ((), (), s32[]{:S(2)}) async-start(), calls=%async_computation.2 | async-start | bytes 2654208 | tf_op jit(solution)/shard_map/all_gather | solution.py:257
  8.8 4.7 %collective-permute-start.18 = (bf16[192,384]{1,0:T(8,128)(2,1)S(1)}, bf16[192,384]{1,0:T(8,128)(2,1)S(1)}, u32[]{:S(2)}, u32[]{:S(2)}) collective-permute-start(bf16[192,384]{1,0:T(8,128)(2,1)S(1)} %bitcast.67), channel_id=1, source_target_pairs={{0,128},{128,0},{1,129},{129,1},{2,130},{130,2},{3,131},{131,3},{4... | collective-permute-start | bytes 442376 | tf_op jit(solution)/shard_map/ppermute | solution.py:256
  14.2 5.6 %copy-start.10 = (bf16[4,128,768]{2,1,0:T(8,128)(2,1)S(1)}, bf16[4,128,768]{2,1,0:T(8,128)(2,1)}, u32[]{:S(2)}) copy-start(bf16[4,128,768]{2,1,0:T(8,128)(2,1)} %param.5) | copy-start | bytes 2359300
  14.2 129.2 %all-gather.8.cloned.1.call-start = ((), (), s32[]{:S(2)}) async-start(), calls=%async_computation.1 | async-start | bytes 2654208 | tf_op jit(solution)/shard_map/all_gather | solution.py:257
  14.5 4.5 %collective-permute-start.13 = (bf16[192,384]{1,0:T(8,128)(2,1)S(1)}, bf16[192,384]{1,0:T(8,128)(2,1)S(1)}, u32[]{:S(2)}, u32[]{:S(2)}) collective-permute-start(bf16[192,384]{1,0:T(8,128)(2,1)S(1)} %bitcast.68), channel_id=1, source_target_pairs={{0,128},{128,0},{1,129},{129,1},{2,130},{130,2},{3,131},{131,3},{4... | collective-permute-start | bytes 442376 | tf_op jit(solution)/shard_map/ppermute | solution.py:256
  19.9 50.8 %copy-start.6 = (bf16[1,128,768]{2,1,0:T(8,128)(2,1)}, bf16[1,128,768]{2,1,0:T(8,128)(2,1)S(1)}, u32[]{:S(2)}) copy-start(bf16[1,128,768]{2,1,0:T(8,128)(2,1)S(1)} %get-tuple-element.15) | copy-start | bytes 589828
  19.9 13.3 %collective-permute-start.5 = (bf16[128,768]{1,0:T(8,128)(2,1)S(1)}, bf16[128,768]{1,0:T(8,128)(2,1)S(1)}, u32[]{:S(2)}, u32[]{:S(2)}) collective-permute-start(bf16[128,768]{1,0:T(8,128)(2,1)S(1)} %get-tuple-element.14), channel_id=1, source_target_pairs={{0,32},{32,64},{64,96},{96,0},{1,33},{33,65},{65,97},{97,1},{2,34}... | collective-permute-start | bytes 589832 | tf_op jit(solution)/shard_map/ppermute | solution.py:239
  23.5 24.2 %collective-permute-start.6 = (bf16[128,768]{1,0:T(8,128)(2,1)S(1)}, bf16[128,768]{1,0:T(8,128)(2,1)S(1)}, u32[]{:S(2)}, u32[]{:S(2)}) collective-permute-start(bf16[128,768]{1,0:T(8,128)(2,1)S(1)} %get-tuple-element.16), channel_id=1, source_target_pairs={{0,64},{32,96},{64,0},{96,32},{1,65},{33,97},{65,1},{97,33},{2,66}... | collective-permute-start | bytes 589832 | tf_op jit(solution)/shard_map/ppermute | solution.py:239
  28.6 20.9 %collective-permute-start.7 = (bf16[128,768]{1,0:T(8,128)(2,1)S(1)}, bf16[128,768]{1,0:T(8,128)(2,1)S(1)}, u32[]{:S(2)}, u32[]{:S(2)}) collective-permute-start(bf16[128,768]{1,0:T(8,128)(2,1)S(1)} %get-tuple-element.13), channel_id=1, source_target_pairs={{0,96},{32,0},{64,32},{96,64},{1,97},{33,1},{65,33},{97,65},{2,98}... | collective-permute-start | bytes 589832 | tf_op jit(solution)/shard_map/ppermute | solution.py:239
  49.6 21.1 %copy-start = (bf16[384,768]{1,0:T(8,128)(2,1)}, bf16[384,768]{1,0:T(8,128)(2,1)S(1)}, u32[]{:S(2)}) copy-start(bf16[384,768]{1,0:T(8,128)(2,1)S(1)} %constant_dynamic-update-slice_fusion.refs_6_) | copy-start | bytes 1769476
  49.6 19.9 %collective-permute-start.8 = (bf16[384,768]{1,0:T(8,128)(2,1)S(1)}, bf16[384,768]{1,0:T(8,128)(2,1)S(1)}, u32[]{:S(2)}, u32[]{:S(2)}) collective-permute-start(bf16[384,768]{1,0:T(8,128)(2,1)S(1)} %constant_dynamic-update-slice_fusion.refs_6_), channel_id=1, source_target_pairs={{0,4},{4,0},{1,5},{5,1},{2,6},{6,2},{3,7},{7,3},{8,12},{12,8},{9,1... | collective-permute-start | bytes 1769480 | tf_op jit(solution)/shard_map/ppermute | solution.py:243
  52.4 14.7 %collective-permute-start = (bf16[128,768]{1,0:T(8,128)(2,1)S(1)}, bf16[128,768]{1,0:T(8,128)(2,1)S(1)}, u32[]{:S(2)}, u32[]{:S(2)}) collective-permute-start(bf16[128,768]{1,0:T(8,128)(2,1)S(1)} %bitcast.61), channel_id=1, source_target_pairs={{0,4},{4,0},{1,5},{5,1},{2,6},{6,2},{3,7},{7,3},{8,12},{12,8},{9,1... | collective-permute-start | bytes 589832 | tf_op jit(solution)/shard_map/ppermute | solution.py:243
  67.1 2.4 copy-start.11
  67.9 37.0 %collective-permute-start.1 = (bf16[2,128,768]{2,1,0:T(8,128)(2,1)}, bf16[2,128,768]{2,1,0:T(8,128)(2,1)}, u32[]{:S(2)}, u32[]{:S(2)}) collective-permute-start(bf16[2,128,768]{2,1,0:T(8,128)(2,1)} %pad_maximum_fusion.1), channel_id=1, source_target_pairs={{0,1},{1,2},{2,3},{3,0},{4,5},{5,6},{6,7},{7,4},{8,9},{9,10},{10,1... | collective-permute-start | bytes 1179656 | tf_op jit(solution)/shard_map/ppermute | solution.py:245
  69.5 1.2 copy-start.3
  70.7 77.3 %collective-permute-start.9 = (bf16[2,384,768]{2,1,0:T(8,128)(2,1)}, bf16[2,384,768]{2,1,0:T(8,128)(2,1)S(1)}, u32[]{:S(2)}, u32[]{:S(2)}) collective-permute-start(bf16[2,384,768]{2,1,0:T(8,128)(2,1)} %pad_maximum_fusion), channel_id=1, source_target_pairs={{0,1},{1,2},{2,3},{3,0},{4,5},{5,6},{6,7},{7,4},{8,9},{9,10},{10,1... | collective-permute-start | bytes 3538952 | tf_op jit(solution)/shard_map/ppermute | solution.py:245
  71.6 84.7 %collective-permute-start.10 = (bf16[2,384,768]{2,1,0:T(8,128)(2,1)}, bf16[2,384,768]{2,1,0:T(8,128)(2,1)S(1)}, u32[]{:S(2)}, u32[]{:S(2)}) collective-permute-start(bf16[2,384,768]{2,1,0:T(8,128)(2,1)} %pad_maximum_fusion), channel_id=1, source_target_pairs={{0,3},{1,0},{2,1},{3,2},{4,7},{5,4},{6,5},{7,6},{8,11},{9,8},{10,9... | collective-permute-start | bytes 3538952 | tf_op jit(solution)/shard_map/ppermute | solution.py:246
  73.5 82.8 %copy-start.7 = (bf16[8,192,384]{2,1,0:T(8,128)(2,1)S(1)}, bf16[8,192,384]{2,1,0:T(8,128)(2,1)}, u32[]{:S(2)}) copy-start(bf16[8,192,384]{2,1,0:T(8,128)(2,1)} %all-gather.6.cloned.1.call-done.refs_0_) | copy-start | bytes 3538948
  73.5 83.9 %collective-permute-start.15 = (bf16[8,192,384]{2,1,0:T(8,128)(2,1)}, bf16[8,192,384]{2,1,0:T(8,128)(2,1)}, u32[]{:S(2)}, u32[]{:S(2)}) collective-permute-start(bf16[8,192,384]{2,1,0:T(8,128)(2,1)} %all-gather.6.cloned.1.call-done.refs_0_), channel_id=1, source_target_pairs={{0,128},{128,0},{1,129},{129,1},{2,130},{130,2},{3,131},{131,3},{4... | collective-permute-start | bytes 3538952 | tf_op jit(solution)/shard_map/ppermute | solution.py:251
  101.3 97.4 %collective-permute-start.19 = (bf16[2,8,192,384]{3,2,1,0:T(8,128)(2,1)}, bf16[2,8,192,384]{3,2,1,0:T(8,128)(2,1)}, u32[]{:S(2)}, u32[]{:S(2)}) collective-permute-start(bf16[2,8,192,384]{3,2,1,0:T(8,128)(2,1)} %bitcast.54), channel_id=1, source_target_pairs={{0,8},{8,0},{1,9},{9,1},{2,10},{10,2},{3,11},{11,3},{4,12},{12,4},... | collective-permute-start | bytes 7077896 | tf_op jit(solution)/shard_map/ppermute | solution.py:258
  104.9 11.4 %collective-permute-start.2 = (bf16[2,128,768]{2,1,0:T(8,128)(2,1)}, bf16[2,128,768]{2,1,0:T(8,128)(2,1)}, u32[]{:S(2)}, u32[]{:S(2)}) collective-permute-start(bf16[2,128,768]{2,1,0:T(8,128)(2,1)} %pad_maximum_fusion.1), channel_id=1, source_target_pairs={{0,3},{1,0},{2,1},{3,2},{4,7},{5,4},{6,5},{7,6},{8,11},{9,8},{10,9... | collective-permute-start | bytes 1179656 | tf_op jit(solution)/shard_map/ppermute | solution.py:246
  116.3 8.0 %collective-permute-start.3 = (bf16[128,768]{1,0:T(8,128)(2,1)S(1)}, bf16[128,768]{1,0:T(8,128)(2,1)}, u32[]{:S(2)}, u32[]{:S(2)}) collective-permute-start(bf16[128,768]{1,0:T(8,128)(2,1)S(1)} %slice_bitcast_fusion.3), channel_id=1, source_target_pairs={{0,1},{1,2},{2,3},{3,0},{4,5},{5,6},{6,7},{7,4},{8,9},{9,10},{10,1... | collective-permute-start | bytes 589832 | tf_op jit(solution)/shard_map/ppermute | solution.py:247
  143.4 92.6 %collective-permute-start.14 = (bf16[2,8,192,384]{3,2,1,0:T(8,128)(2,1)}, bf16[2,8,192,384]{3,2,1,0:T(8,128)(2,1)}, u32[]{:S(2)}, u32[]{:S(2)}) collective-permute-start(bf16[2,8,192,384]{3,2,1,0:T(8,128)(2,1)} %bitcast.56), channel_id=1, source_target_pairs={{0,8},{8,0},{1,9},{9,1},{2,10},{10,2},{3,11},{11,3},{4,12},{12,4},... | collective-permute-start | bytes 7077896 | tf_op jit(solution)/shard_map/ppermute | solution.py:258
  148.0 10.4 %copy-start.1 = (bf16[2,384,768]{2,1,0:T(8,128)(2,1)}, bf16[2,384,768]{2,1,0:T(8,128)(2,1)S(1)}, u32[]{:S(2)}) copy-start(bf16[2,384,768]{2,1,0:T(8,128)(2,1)S(1)} %collective-permute-done.9.refs_8_) | copy-start | bytes 3538948
  148.0 7.2 %collective-permute-start.4 = (bf16[128,768]{1,0:T(8,128)(2,1)S(1)}, bf16[128,768]{1,0:T(8,128)(2,1)}, u32[]{:S(2)}, u32[]{:S(2)}) collective-permute-start(bf16[128,768]{1,0:T(8,128)(2,1)S(1)} %slice_bitcast_fusion.2), channel_id=1, source_target_pairs={{0,3},{1,0},{2,1},{3,2},{4,7},{5,4},{6,5},{7,6},{8,11},{9,8},{10,9... | collective-permute-start | bytes 589832 | tf_op jit(solution)/shard_map/ppermute | solution.py:248
  155.2 16.4 %collective-permute-start.11 = (bf16[384,768]{1,0:T(8,128)(2,1)S(1)}, bf16[384,768]{1,0:T(8,128)(2,1)S(1)}, u32[]{:S(2)}, u32[]{:S(2)}) collective-permute-start(bf16[384,768]{1,0:T(8,128)(2,1)S(1)} %slice_bitcast_fusion.1), channel_id=1, source_target_pairs={{0,1},{1,2},{2,3},{3,0},{4,5},{5,6},{6,7},{7,4},{8,9},{9,10},{10,1... | collective-permute-start | bytes 1769480 | tf_op jit(solution)/shard_map/ppermute | solution.py:247
  156.3 29.9 %copy-start.2 = (bf16[2,384,768]{2,1,0:T(8,128)(2,1)}, bf16[2,384,768]{2,1,0:T(8,128)(2,1)S(1)}, u32[]{:S(2)}) copy-start(bf16[2,384,768]{2,1,0:T(8,128)(2,1)S(1)} %collective-permute-done.10.refs_9_) | copy-start | bytes 3538948
  156.3 42.4 %collective-permute-start.16 = (bf16[8,192,384]{2,1,0:T(8,128)(2,1)S(1)}, bf16[8,192,384]{2,1,0:T(8,128)(2,1)}, u32[]{:S(2)}, u32[]{:S(2)}) collective-permute-start(bf16[8,192,384]{2,1,0:T(8,128)(2,1)S(1)} %copy-done.7), channel_id=1, source_target_pairs={{0,8},{8,0},{1,9},{9,1},{2,10},{10,2},{3,11},{11,3},{4,12},{12,4},... | collective-permute-start | bytes 3538952 | tf_op jit(solution)/shard_map/ppermute | solution.py:252
  157.4 41.3 %collective-permute-start.17 = (bf16[8,192,384]{2,1,0:T(8,128)(2,1)}, bf16[8,192,384]{2,1,0:T(8,128)(2,1)}, u32[]{:S(2)}, u32[]{:S(2)}) collective-permute-start(bf16[8,192,384]{2,1,0:T(8,128)(2,1)} %collective-permute-done.15.refs_1_), channel_id=1, source_target_pairs={{0,8},{8,0},{1,9},{9,1},{2,10},{10,2},{3,11},{11,3},{4,12},{12,4},... | collective-permute-start | bytes 3538952 | tf_op jit(solution)/shard_map/ppermute | solution.py:253
  171.6 0.9 copy-start.12
  172.5 13.7 %collective-permute-start.12 = (bf16[384,768]{1,0:T(8,128)(2,1)}, bf16[384,768]{1,0:T(8,128)(2,1)S(1)}, u32[]{:S(2)}, u32[]{:S(2)}) collective-permute-start(bf16[384,768]{1,0:T(8,128)(2,1)} %slice_bitcast_fusion), channel_id=1, source_target_pairs={{0,3},{1,0},{2,1},{3,2},{4,7},{5,4},{6,5},{7,6},{8,11},{9,8},{10,9... | collective-permute-start | bytes 1769480 | tf_op jit(solution)/shard_map/ppermute | solution.py:248
  186.2 0.9 copy-start.13
  213.6 17.1 %collective-permute-start.20 = (bf16[512,768]{1,0:T(8,128)(2,1)}, bf16[512,768]{1,0:T(8,128)(2,1)S(1)}, u32[]{:S(2)}, u32[]{:S(2)}) collective-permute-start(bf16[512,768]{1,0:T(8,128)(2,1)} %shard_map.57.refs_1_), channel_id=1, source_target_pairs={{0,128},{128,0},{1,129},{129,1},{2,130},{130,2},{3,131},{131,3},{4... | collective-permute-start | bytes 2359304 | tf_op jit(solution)/shard_map/ppermute | solution.py:265
  214.7 20.2 %collective-permute-start.21 = (bf16[512,768]{1,0:T(8,128)(2,1)}, bf16[512,768]{1,0:T(8,128)(2,1)S(1)}, u32[]{:S(2)}, u32[]{:S(2)}) collective-permute-start(bf16[512,768]{1,0:T(8,128)(2,1)} %shard_map.57.refs_1_), channel_id=1, source_target_pairs={{0,16},{16,0},{1,17},{17,1},{2,18},{18,2},{3,19},{19,3},{4,20},{20... | collective-permute-start | bytes 2359304 | tf_op jit(solution)/shard_map/ppermute | solution.py:266
  215.7 53.7 %collective-permute-start.24 = (bf16[512,768]{1,0:T(8,128)(2,1)}, bf16[512,768]{1,0:T(8,128)(2,1)S(1)}, u32[]{:S(2)}, u32[]{:S(2)}) collective-permute-start(bf16[512,768]{1,0:T(8,128)(2,1)} %shard_map.57.refs_1_), channel_id=1, source_target_pairs={{0,8},{8,0},{1,9},{9,1},{2,10},{10,2},{3,11},{11,3},{4,12},{12,4},... | collective-permute-start | bytes 2359304 | tf_op jit(solution)/shard_map/ppermute | solution.py:271
  230.6 38.7 %copy-start.4 = (bf16[512,768]{1,0:T(8,128)(2,1)}, bf16[512,768]{1,0:T(8,128)(2,1)S(1)}, u32[]{:S(2)}) copy-start(bf16[512,768]{1,0:T(8,128)(2,1)S(1)} %collective-permute-done.20.refs_2_) | copy-start | bytes 2359300
  230.6 9.7 %collective-permute-start.22 = (bf16[256,768]{1,0:T(8,128)(2,1)S(1)}, bf16[256,768]{1,0:T(8,128)(2,1)S(1)}, u32[]{:S(2)}, u32[]{:S(2)}) collective-permute-start(bf16[256,768]{1,0:T(8,128)(2,1)S(1)} %slice.40), channel_id=1, source_target_pairs={{0,16},{16,0},{1,17},{17,1},{2,18},{18,2},{3,19},{19,3},{4,20},{20... | collective-permute-start | bytes 1179656 | tf_op jit(solution)/shard_map/ppermute | solution.py:268
  231.5 37.9 %collective-permute-start.25 = (bf16[512,768]{1,0:T(8,128)(2,1)S(1)}, bf16[512,768]{1,0:T(8,128)(2,1)S(1)}, u32[]{:S(2)}, u32[]{:S(2)}) collective-permute-start(bf16[512,768]{1,0:T(8,128)(2,1)S(1)} %collective-permute-done.20.refs_2_), channel_id=1, source_target_pairs={{0,8},{8,0},{1,9},{9,1},{2,10},{10,2},{3,11},{11,3},{4,12},{12,4},... | collective-permute-start | bytes 2359304 | tf_op jit(solution)/shard_map/ppermute | solution.py:271
  235.0 34.4 %copy-start.5 = (bf16[512,768]{1,0:T(8,128)(2,1)}, bf16[512,768]{1,0:T(8,128)(2,1)S(1)}, u32[]{:S(2)}) copy-start(bf16[512,768]{1,0:T(8,128)(2,1)S(1)} %collective-permute-done.21.refs_3_) | copy-start | bytes 2359300
  235.0 34.4 %collective-permute-start.26 = (bf16[512,768]{1,0:T(8,128)(2,1)S(1)}, bf16[512,768]{1,0:T(8,128)(2,1)}, u32[]{:S(2)}, u32[]{:S(2)}) collective-permute-start(bf16[512,768]{1,0:T(8,128)(2,1)S(1)} %collective-permute-done.21.refs_3_), channel_id=1, source_target_pairs={{0,8},{8,0},{1,9},{9,1},{2,10},{10,2},{3,11},{11,3},{4,12},{12,4},... | collective-permute-start | bytes 2359304 | tf_op jit(solution)/shard_map/ppermute | solution.py:271
  236.0 10.8 %collective-permute-start.23 = (bf16[256,768]{1,0:T(8,128)(2,1)S(1)}, bf16[256,768]{1,0:T(8,128)(2,1)}, u32[]{:S(2)}, u32[]{:S(2)}) collective-permute-start(bf16[256,768]{1,0:T(8,128)(2,1)S(1)} %slice.41), channel_id=1, source_target_pairs={{0,128},{128,0},{1,129},{129,1},{2,130},{130,2},{3,131},{131,3},{4... | collective-permute-start | bytes 1179656 | tf_op jit(solution)/shard_map/ppermute | solution.py:269
  240.4 29.0 %copy-start.14 = (bf16[256,768]{1,0:T(8,128)(2,1)}, bf16[256,768]{1,0:T(8,128)(2,1)S(1)}, u32[]{:S(2)}) copy-start(bf16[256,768]{1,0:T(8,128)(2,1)S(1)} %collective-permute-done.22.refs_4_) | copy-start | bytes 1179652
  240.4 29.0 %collective-permute-start.27 = (bf16[256,768]{1,0:T(8,128)(2,1)S(1)}, bf16[256,768]{1,0:T(8,128)(2,1)}, u32[]{:S(2)}, u32[]{:S(2)}) collective-permute-start(bf16[256,768]{1,0:T(8,128)(2,1)S(1)} %collective-permute-done.22.refs_4_), channel_id=1, source_target_pairs={{0,8},{8,0},{1,9},{9,1},{2,10},{10,2},{3,11},{11,3},{4,12},{12,4},... | collective-permute-start | bytes 1179656 | tf_op jit(solution)/shard_map/ppermute | solution.py:271
  246.8 22.6 %collective-permute-start.28 = (bf16[256,768]{1,0:T(8,128)(2,1)}, bf16[256,768]{1,0:T(8,128)(2,1)}, u32[]{:S(2)}, u32[]{:S(2)}) collective-permute-start(bf16[256,768]{1,0:T(8,128)(2,1)} %collective-permute-done.23.refs_5_), channel_id=1, source_target_pairs={{0,8},{8,0},{1,9},{9,1},{2,10},{10,2},{3,11},{11,3},{4,12},{12,4},... | collective-permute-start | bytes 1179656 | tf_op jit(solution)/shard_map/ppermute | solution.py:271
  269.4 0.9 copy-start.8
  269.4 1.2 copy-start.9
  286.4 7.4 %collective-permute-start.29 = (bf16[128,384]{1,0:T(8,128)(2,1)}, bf16[128,384]{1,0:T(8,128)(2,1)S(1)}, u32[]{:S(2)}, u32[]{:S(2)}) collective-permute-start(bf16[128,384]{1,0:T(8,128)(2,1)} %get-tuple-element.10), channel_id=1, source_target_pairs={{0,96},{32,0},{64,32},{96,64},{1,97},{33,1},{65,33},{97,65},{2,98}... | collective-permute-start | bytes 294920 | tf_op jit(solution)/shard_map/ppermute | solution.py:273
  289.7 11.1 %collective-permute-start.30 = (bf16[128,384]{1,0:T(8,128)(2,1)}, bf16[128,384]{1,0:T(8,128)(2,1)S(1)}, u32[]{:S(2)}, u32[]{:S(2)}) collective-permute-start(bf16[128,384]{1,0:T(8,128)(2,1)} %get-tuple-element.11), channel_id=1, source_target_pairs={{0,64},{32,96},{64,0},{96,32},{1,65},{33,97},{65,1},{97,33},{2,66}... | collective-permute-start | bytes 294920 | tf_op jit(solution)/shard_map/ppermute | solution.py:273
  292.4 8.3 %collective-permute-start.31 = (bf16[128,384]{1,0:T(8,128)(2,1)}, bf16[128,384]{1,0:T(8,128)(2,1)S(1)}, u32[]{:S(2)}, u32[]{:S(2)}) collective-permute-start(bf16[128,384]{1,0:T(8,128)(2,1)} %get-tuple-element.12), channel_id=1, source_target_pairs={{0,32},{32,64},{64,96},{96,0},{1,33},{33,65},{65,97},{97,1},{2,34}... | collective-permute-start | bytes 294920 | tf_op jit(solution)/shard_map/ppermute | solution.py:273
Sparse Core Ops, SparseCore 0:
  9.1 50.6 all-gather.5
  61.6 39.5 all-gather.9
  103.1 40.2 all-gather.7

commit v2 on v0

v2 whole, which is shorter than its diff:
```python
import jax
import jax.numpy as jnp
from jax import lax
from jax.experimental import pallas as pl
from jax.experimental.pallas import tpu as pltpu
from jax.sharding import Mesh, PartitionSpec as P

TP = 8
KB = 768
SUB = 192
HD = 128
W = 384
SWAP = [(0, 1), (1, 0)]
VMEM_LIMIT = 58 * 1024 * 1024
ANY = pl.BlockSpec(memory_space=pl.ANY)
VM = pl.BlockSpec(memory_space=pltpu.VMEM)
BF, F32 = jnp.bfloat16, jnp.float32


def ring(n, shift):
    return [(i, (i + shift) % n) for i in range(n)]


def after(value, *others):
    return lax.optimization_barrier((value,) + others)[0]


def call(kernel, outs, ins, scratch, flops, moved):
    return pl.pallas_call(
        kernel,
        out_shape=outs,
        in_specs=ins,
        out_specs=[VM] * len(outs),
        scratch_shapes=scratch,
        cost_estimate=pl.CostEstimate(flops=flops, transcendentals=0, bytes_accessed=moved),
        compiler_params=pltpu.CompilerParams(vmem_limit_bytes=VMEM_LIMIT),
    )


def norm_kernel(c0, c1, f, b, g, h, gain_ref, out_ref, held, sems):
    xh, y = lax.axis_index("xh"), lax.axis_index("y")
    plan = (
        (c0, 0, 0), (c1, 1, 0), (f.at[0], 0, 3), (f.at[1], 1, 3),
        (b.at[0], 0, 1), (b.at[1], 1, 1), (g, 0, 2), (h, 1, 2),
    )
    copies = []
    for src, dx, dy in plan:
        t = lax.rem(xh + dx, 2) * 4 + lax.rem(y + dy, 4)
        copies.append(pltpu.make_async_copy(src, held.at[t], sems.at[len(copies)]))
    for copy in copies:
        copy.start()
    for copy in copies:
        copy.wait()
    tile = 16

    def rows_step(i, carry):
        r = pl.multiple_of(i * tile, tile)
        part = jnp.zeros((tile, 128), F32)
        part2 = jnp.zeros((tile, 128), F32)
        for t in range(TP):
            block = held[t, pl.ds(r, tile), :].astype(F32)
            for j in range(KB // 128):
                piece = block[:, j * 128 : (j + 1) * 128]
                part = part + piece
                part2 = part2 + piece * piece
        center = jnp.sum(part, axis=-1, keepdims=True) * (1.0 / (TP * KB))
        spread = jnp.sum(part2, axis=-1, keepdims=True) * (1.0 / (TP * KB)) - center * center
        scale = lax.rsqrt(spread + 1e-06)
        for t in range(TP):
            xl, zh = t // 4, t % 4
            block = held[t, pl.ds(r, tile), :].astype(F32)
            block = ((block - center) * scale * gain_ref[t : t + 1, :]).astype(BF)
            for zl in range(2):
                out_ref[2 * zh + zl, pl.ds(r, tile), xl * W : (xl + 1) * W] = block[:, zl * W : (zl + 1) * W]
        return carry

    lax.fori_loop(0, held.shape[1] // tile, rows_step, 0)


def norm_rows(pieces, gain):
    rows = pieces[0].shape[0]
    return call(
        norm_kernel,
        [jax.ShapeDtypeStruct((8, rows, KB), BF)],
        [ANY] * 6 + [VM],
        [pltpu.VMEM((TP, rows, KB), BF), pltpu.SemaphoreType.DMA((8,))],
        rows * 6144 * 12,
        rows * 6144 * 4,
    )(*pieces, gain)[0]


def head_norm(values_in, gain):
    center = jnp.mean(values_in, axis=-1, keepdims=True)
    spread = jnp.mean(values_in * values_in, axis=-1, keepdims=True) - center * center
    return (values_in - center) * lax.rsqrt(spread + 1e-06) * gain


def product_call(blocks, normed, begun, arrays, gain, col, width):
    n, m = len(blocks), len(arrays)

    def kernel(x_own, x_rest, *refs):
        refs = list(refs)
        begun_ref = refs.pop(0) if begun is not None else None
        sources, refs = refs[:m], refs[m:]
        gain_ref = refs.pop(0) if gain is not None else None
        out, xbuf, wbuf, sems, sem = refs[0], refs[-4], refs[-3], refs[-2], refs[-1]
        total = out if gain is None else refs[1]
        xl, core = lax.axis_index("xl"), lax.axis_index("core")
        z = 2 * lax.axis_index("zh") + lax.axis_index("zl")
        if begun is not None:
            first = pltpu.make_async_copy(begun_ref.at[:, pl.ds(col, width)], total, sem)
            first.start()

        def weight_copy(source, k, dx, dc):
            return pltpu.make_async_copy(
                source.at[:, pl.ds(col, width)],
                wbuf.at[k, lax.rem(xl + dx, 2), lax.rem(core + dc, 2)],
                sems.at[k, 2 + 2 * dx + dc],
            )

        def rows_copies(at, k):
            return (
                pltpu.make_async_copy(x_own.at[at], xbuf.at[k, 0:128, :], sems.at[k, 0]),
                pltpu.make_async_copy(x_rest.at[at], xbuf.at[k, 128:512, :], sems.at[k, 1]),
            )

        like = None
        for k, (up, down, find) in enumerate(blocks):
            at = lax.rem(z + 8 + up + core * (down - up), 8)
            for copy in rows_copies(at, k):
                copy.start()
            for dx in range(2):
                for dc in range(2):
                    i, index = find(dc, dx)
                    like = sources[i].at[index]
                    weight_copy(like, k, dx, dc).start()
        if begun is None:
            total[...] = jnp.zeros_like(total)
        else:
            first.wait()

        def step(k, carry):
            for copy in rows_copies(0, k):
                copy.wait()
            for dx in range(2):
                for dc in range(2):
                    weight_copy(like, k, dx, dc).wait()
            total[...] += jnp.dot(xbuf[k], wbuf[k].reshape(KB, width), preferred_element_type=F32)
            return carry

        lax.fori_loop(0, n, step, 0)
        if gain is not None:
            for h in range(3):
                cols = slice(h * HD, (h + 1) * HD)
                out[:, cols] = head_norm(total[:, cols], gain_ref[h : h + 1, :]).astype(BF)
            if width > W:
                out[:, W:] = total[:, W:].astype(BF)

    args = [*normed, *(() if begun is None else (begun,)), *arrays, *(() if gain is None else (gain,))]
    return call(
        kernel,
        [jax.ShapeDtypeStruct((512, width), F32 if gain is None else BF)],
        [ANY] * (len(args) - (gain is not None)) + [VM] * (gain is not None),
        ([] if gain is None else [pltpu.VMEM((512, width), F32)])
        + [
            pltpu.VMEM((n, 512, KB), BF),
            pltpu.VMEM((n, 2, 2, SUB, width), BF),
            pltpu.SemaphoreType.DMA((n, 6)),
            pltpu.SemaphoreType.DMA,
        ],
        n * 2 * 512 * KB * width,
        n * (512 * KB + KB * width) * 2 + 512 * width * 8,
    )(*args)[0]


def both_cores(i, s):
    return [
        (-s, s, lambda dc, dx: (i, (dc, dx))),
        (s, -s, lambda dc, dx: (i + 1, (1 - dc, dx))),
    ]


SCALE = 1.0 / (HD ** 0.5)


def attend(queries, state, parts, last):
    n, keys_n = len(parts), sum(part.shape[0] for part in parts)
    begins = state is None

    def kernel(q_ref, *refs):
        refs = list(refs)
        old = None if begins else (refs.pop(0), refs.pop(0))
        sources, refs = refs[:n], refs[n:]
        outs, held, sems = refs[:-2], refs[-2], refs[-1]
        row, copies = 0, []
        for i, source in enumerate(sources):
            rows = source.shape[0]
            copies.append(pltpu.make_async_copy(source, held.at[pl.ds(row, rows), :], sems.at[i]))
            row += rows
        for copy in copies:
            copy.start()
        for copy in copies:
            copy.wait()
        zh = lax.axis_index("zh")
        tile = 256

        def head(h, carry):
            cols = pl.ds(pl.multiple_of(h * HD, HD), HD)
            value_cols = pl.ds(pl.multiple_of(W + h * HD, HD), HD)
            keys, values = held[:, cols], held[:, value_cols]
            for part in range(512 // tile):
                rows = slice(part * tile, part * tile + tile)
                scores = lax.dot_general(
                    q_ref[rows, cols], keys, (((1,), (1,)), ((), ())), preferred_element_type=F32
                ) * SCALE
                best = jnp.max(scores, axis=-1, keepdims=True)
                if not begins:
                    before = old[1][h, rows, 0:1]
                    best = jnp.maximum(best, before)
                expd = jnp.exp(scores - best)
                totals = jnp.sum(expd, axis=-1, keepdims=True)
                summed = jnp.dot(expd.astype(BF), values, preferred_element_type=F32)
                if not begins:
                    keep = jnp.exp(before - best)
                    totals = totals + keep * old[1][h, rows, 1:2]
                    summed = summed + keep * old[0][rows, cols]
                if last:
                    result = (summed / totals).astype(BF)
                    for s in range(part * tile // 128, (part + 1) * tile // 128):
                        here = slice(s * 128 - part * tile, s * 128 + 128 - part * tile)
                        outs[0][lax.rem(zh + s, 4), :, cols] = result[here]
                else:
                    outs[0][rows, cols] = summed
                    outs[1][h, rows, 0:1] = best
                    outs[1][h, rows, 1:2] = totals
            return carry

        lax.fori_loop(0, 3, head, 0)

    if last:
        out_shape = [jax.ShapeDtypeStruct((4, 128, W), BF)]
    else:
        out_shape = [jax.ShapeDtypeStruct((512, W), F32), jax.ShapeDtypeStruct((3, 512, HD), F32)]
    return call(
        kernel,
        out_shape,
        [VM] * (1 if begins else 3) + [ANY] * n,
        [pltpu.VMEM((keys_n, 2 * W), BF), pltpu.SemaphoreType.DMA((n,))],
        512 * keys_n * 3 * HD * 8,
        keys_n * 2 * W * 2 + 512 * W * 8,
    )(queries, *(() if begins else state), *parts)


def shards(patches, ln_gain, w_qkv, query_gain, key_gain):
    zh = lax.axis_index("zh")
    gain = ln_gain.reshape(TP, KB)

    def send(value, axis, n, shift):
        return lax.ppermute(value, axis, ring(n, shift))

    def swap(value, axis):
        return lax.ppermute(value, axis, SWAP)

    both_ways = [(2 * z + c, 2 * ((z + (1, -1)[c]) % 8) + c) for z in range(8) for c in range(2)]

    def send_z(value):
        return lax.ppermute(value, ("zh", "zl", "core"), both_ways)

    weight = w_qkv.reshape(SUB, 3 * W)
    mine = lax.dynamic_index_in_dim(patches, zh, 0, keepdims=False)
    mine_x = swap(mine, "xh")
    weight_x = swap(weight, "xl")
    crops = lax.all_to_all(patches, "zh", 0, 0, tiled=True)
    crops = jnp.concatenate([crops, crops[:3]])
    rest = lax.dynamic_slice_in_dim(crops, zh + 1, 3, axis=0).reshape(384, KB)
    rest_x = swap(rest, "xh")
    w0 = jnp.stack([weight, weight_x])
    w0_c = swap(after(w0, rest), "core")
    mine_pair = after(jnp.stack([mine, mine_x]), rest)
    mine_f, mine_b = send(mine_pair, "y", 4, 1), send(mine_pair, "y", 4, -1)
    w0_both = jnp.stack([w0, w0_c])
    r1 = send_z(w0_both)
    mine_g, mine_h = send(mine_f[0], "y", 4, 1), send(mine_b[1], "y", 4, -1)
    normed_mine = norm_rows((mine, mine_x, mine_f, mine_b, mine_g, mine_h), gain)
    rest_pair = after(jnp.stack([rest, rest_x]), mine_g, mine_h)
    rest_f, rest_b = send(rest_pair, "y", 4, 1), send(rest_pair, "y", 4, -1)
    r1 = after(r1, rest_pair, normed_mine)
    r2, r1_c = send_z(r1), swap(r1, "core")
    rest_g, rest_h = send(rest_f[0], "y", 4, 1), send(rest_b[1], "y", 4, -1)
    r2 = after(r2, r1_c, rest_f, rest_b)
    r3, r2_c = send_z(r2), swap(r2, "core")
    normed_rest = norm_rows((rest, rest_x, rest_f, rest_b, rest_g, rest_h), gain)
    r3 = after(r3, r2_c, normed_rest)
    r4, r3_c = send_z(r3[0]), swap(r3, "core")
    normed = (normed_mine, normed_rest)
    first = [(0, 0, lambda dc, dx: (0, (dc, dx)))] + both_cores(1, 1) + both_cores(3, 2)
    begun = product_call(first, normed, None, (w0_both, r1, r1_c, r2, r2_c), None, 0, 3 * W)
    begun = product_call(both_cores(0, 3), normed, after(begun, r3_c), (r3, r3_c), None, 0, 3 * W)
    r4 = after(r4, begun)
    r4_c = swap(r4, "core")
    final = [(4, 4, lambda dc, dx: (dc, dx))]
    near = product_call(final, normed, begun, (r4, r4_c), key_gain, W, 2 * W)

    across_x, across_z, near_c = swap(near, "xl"), swap(near, "zl"), swap(near, "core")
    queries = product_call(final, normed, begun, (r4, r4_c), query_gain, 0, W)
    state = attend(queries, None, (near, near_c), False)
    across_x, across_z = after(across_x, state[1]), after(across_z, state[1])
    diag0, diag1 = swap(across_x[:256], "zl"), swap(across_z[256:], "xl")
    across_x_c, across_z_c = swap(across_x, "core"), swap(across_z, "core")
    state = attend(queries, state, (across_x, across_z, across_x_c, across_z_c), False)
    diag0, diag1 = after(diag0, state[1]), after(diag1, state[1])
    diag0_c, diag1_c = swap(diag0, "core"), swap(diag1, "core")
    (out,) = attend(queries, state, (diag0, diag1, diag0_c, diag1_c), True)
    out = lax.all_to_all(out, "zh", 0, 0, tiled=True)
    return out.reshape(4, 128, 3, HD)


def solution(mesh):
    fine = Mesh(mesh.devices.reshape(2, 4, 2, 2, 2, 4), ("xl", "zh", "zl", "core", "xh", "y"))
    ctx, tp = ("xl", "zh", "zl", "core"), ("xh", "y")
    return jax.shard_map(
        shards,
        mesh=fine,
        in_specs=(P(None, ctx, tp), P(), P(ctx, None, tp, None), P(tp, None), P(tp, None)),
        out_specs=P(None, ctx, tp, None),
        check_vma=False,
    )
```

time: 525 us -> 228 us (0.43)
  waiting for transfers between devices: 418 us -> 71.9 us
  Pallas kernels: 0 us -> 66.8 us
  matrix products: 53.1 us -> 0 us
  starting transfers between devices: 0.38 us -> 50.5 us
  blocking collectives: 0 us -> 17.4 us
  other arithmetic: 17 us -> 3.72 us
  between operations: 13.5 us -> 0.38 us
  local copies, waits for them, and re-layouts: 21.8 us -> 15.8 us
    all_gather x6 -> x0, waiting for transfers between devices: 416 us -> none  [the longest x1 95.4 us: shards(): key_block = lax.all_gather(keys_local, 'ctx', axis=1, tiled=True)]
    ppermute x0 -> x29, waiting for transfers between devices: none -> 68.3 us  [the longest x8 42.2 us: send(): return lax.ppermute(value, axis, ring(n, shift))]
    pallas_call x0 -> x9, Pallas kernels: none -> 66.8 us  [the longest x3 26.4 us: attend(): call(kernel, out_shape, [VM] * (1 if begins else 3) + [ANY] * n, [pltpu.V...]
    dot_general x5 -> x0, matrix products: 53.1 us -> none  [the longest x3 20.9 us: add_panel(): jnp.dot(normed_rows, panel.reshape(panel.shape[0], -1), preferred_element...]
    ppermute x0 -> x29, starting transfers between devices: none -> 41.4 us  [the longest x17 23.4 us: swap(): return lax.ppermute(value, axis, SWAP)]
    all_gather x3 -> x0, local copies, waits for them, and re-layouts: 20 us -> none  [the longest x1 6.68 us: shards(): lax.all_gather(w_qkv[:, 0], 'ctx', axis=0, tiled=True)]
    all_to_all x0 -> x1, blocking collectives: none -> 17.4 us  [shards(): out = lax.all_to_all(out, 'zh', 0, 0, tiled=True)]
    reduce_sum x2 -> x0, other arithmetic: 16 us -> none  [the longest x1 11.2 us: shards(): totals = totals * correction + jnp.sum(expd, axis=-1)]
  transfers between devices with their start and end apart: 6 -> 30, of which waited for: 6 -> 15; matrix products, arithmetic and copies ran while one was open for 14% -> 4% of each run, Pallas kernels for 0% -> 24%
where the time goes in v2:
time: 228 us; the launch traced here: 227 us
  waiting for transfers between devices  71.9 us (32%)
  Pallas kernels  66.8 us (29%)
  starting transfers between devices  50.5 us (22%)
  blocking collectives  17.4 us (8%)
  local copies, waits for them, and re-layouts  15.8 us (7%)
  other arithmetic  3.72 us (2%)
    ppermute x8, waiting for transfers between devices, send(): return lax.ppermute(value, axis, ring(n, shift))  42.2 us
    pallas_call x3, Pallas kernels, attend(): call(kernel, out_shape, [VM] * (1 if begins else 3) + [ANY] * n, [pltpu.V...  26.4 us
    ppermute x17, waiting for transfers between devices, swap(): return lax.ppermute(value, axis, SWAP)  26.1 us
    pallas_call x4, Pallas kernels, product_call(): call(kernel, [jax.ShapeDtypeStruct((512, width), F32 if gain is None else...  25 us
    ppermute x17, starting transfers between devices, swap(): return lax.ppermute(value, axis, SWAP)  23.4 us
    all_to_all x1, blocking collectives, shards(): out = lax.all_to_all(out, 'zh', 0, 0, tiled=True)  17.4 us
    pallas_call x2, Pallas kernels, norm_rows(): call(norm_kernel, [jax.ShapeDtypeStruct((8, rows, KB), BF)], [ANY] * 6 +...  15.4 us
    ppermute x8, starting transfers between devices, send(): return lax.ppermute(value, axis, ring(n, shift))  12 us
  transfers between devices with their start and end apart: 30, of which 15 were waited for; matrix products, arithmetic and copies ran while one was open for 4% of the time, Pallas kernels for 24%

profile of v2, /device:TPU:1, one launch (start us, length us, event | category | flops | bytes accessed | tf_op | source)
XLA Modules:
  0.0 226.5 jit_solution(10425160103623604939)
XLA Ops:
  0.0 9.1 %all-to-all-start = ((bf16[4,128,768]{2,1,0:T(8,128)(2,1)}), bf16[4,128,768]{2,1,0:T(8,128)(2,1)S(1)}, u32[]{:S(2)}, u32[]{:S(2)}) async-start(bf16[4,128,768]{2,1,0:T(8,128)(2,1)} %param.5), calls=%async_computation | async-start | bytes 1572864 | tf_op jit(solution)/shard_map/all_to_all | solution.py:273
  9.9 1.3 collective-permute-start.10
  11.6 9.1 %collective-permute-done.10 = bf16[192,1152]{1,0:T(8,128)(2,1)S(1)} collective-permute-done((bf16[192,1152]{1,0:T(8,128)(2,1)S(1)}, bf16[192,1152]{1,0:T(8,128)(2,1)S(1)}, u32[]{:S(2)}, u32[]{:S(2)}) %collective-permute-start.10) | collective-permute-done | bytes 442400 | tf_op jit(solution)/shard_map/ppermute | solution.py:262
  20.7 0.8 copy-done.18
  21.5 2.1 fusion.1
  23.6 3.6 %all-to-all-done = bf16[4,128,768]{2,1,0:T(8,128)(2,1)S(1)} async-done(((bf16[4,128,768]{2,1,0:T(8,128)(2,1)}), bf16[4,128,768]{2,1,0:T(8,128)(2,1)S(1)}, u32[]{:S(2)}, u32[]{:S(2)}) %all-to-all-start) | async-done | bytes 786464 | tf_op jit(solution)/shard_map/all_to_all | solution.py:273
  27.5 0.9 copy-done.13
  28.3 1.7 collective-permute-start.11
  30.1 2.1 collective-permute-done.11
  32.3 2.2 collective-permute-start.12
  34.5 0.9 fusion.2.c0
  35.5 2.8 %collective-permute-start = (bf16[128,768]{1,0:T(8,128)(2,1)S(1)}, bf16[128,768]{1,0:T(8,128)(2,1)S(1)}, u32[]{:S(2)}, u32[]{:S(2)}) collective-permute-start(bf16[128,768]{1,0:T(8,128)(2,1)S(1)} %fusion.2.c0), channel_id=1, source_target_pairs={{0,4},{4,0},{1,5},{5,1},{2,6},{6,2},{3,7},{7,3},{8,12},{12,8},{9,1... | collective-permute-start | bytes 589832 | tf_op jit(solution)/shard_map/ppermute | solution.py:262
  38.3 0.9 constant_dynamic-slice_fusion
  39.3 2.3 %collective-permute-done.c1 = bf16[128,768]{1,0:T(8,128)(2,1)S(1)} collective-permute-done((bf16[128,768]{1,0:T(8,128)(2,1)S(1)}, bf16[128,768]{1,0:T(8,128)(2,1)S(1)}, u32[]{:S(2)}, u32[]{:S(2)}) %collective-permute-start) | collective-permute-done | bytes 196640 | tf_op jit(solution)/shard_map/ppermute | solution.py:262
  41.6 0.7 copy-done.15
  42.3 1.4 collective-permute-start.1
  43.7 1.5 collective-permute-start.2
  45.2 3.1 %collective-permute-start.5 = (bf16[384,768]{1,0:T(8,128)(2,1)S(1)}, bf16[384,768]{1,0:T(8,128)(2,1)S(1)}, u32[]{:S(2)}, u32[]{:S(2)}) collective-permute-start(bf16[384,768]{1,0:T(8,128)(2,1)S(1)} %bitcast.21), channel_id=1, source_target_pairs={{0,4},{4,0},{1,5},{5,1},{2,6},{6,2},{3,7},{7,3},{8,12},{12,8},{9,1... | collective-permute-start | bytes 1769480 | tf_op jit(solution)/shard_map/ppermute | solution.py:262
  48.4 2.3 %collective-permute-done.1.f = bf16[2,128,768]{2,1,0:T(8,128)(2,1)S(1)} collective-permute-done((bf16[2,128,768]{2,1,0:T(8,128)(2,1)S(1)}, bf16[2,128,768]{2,1,0:T(8,128)(2,1)S(1)}, u32[]{:S(2)}, u32[]{:S(2)}) %collective-permute-start.1) | collective-permute-done | bytes 393248 | tf_op jit(solution)/shard_map/ppermute | solution.py:259
  50.7 0.7 slice_bitcast_fusion.4
  51.4 0.7 copy-done.12
  52.2 0.7 slice_bitcast_fusion.3
  52.9 2.7 %collective-permute-start.4 = (bf16[128,768]{1,0:T(8,128)(2,1)}, bf16[128,768]{1,0:T(8,128)(2,1)}, u32[]{:S(2)}, u32[]{:S(2)}) collective-permute-start(bf16[128,768]{1,0:T(8,128)(2,1)} %slice_bitcast_fusion.3), channel_id=1, source_target_pairs={{0,3},{1,0},{2,1},{3,2},{4,7},{5,4},{6,5},{7,6},{8,11},{9,8},{10,9... | collective-permute-start | bytes 589832 | tf_op jit(solution)/shard_map/ppermute | solution.py:259
  55.5 1.3 reshape.13.gain_ref
  57.3 1.2 pad_maximum_fusion.1
  58.5 5.1 %shard_map.55.x_own = bf16[8,128,768]{2,1,0:T(8,128)(2,1)} custom-call(bf16[128,768]{1,0:T(8,128)(2,1)} %copy-done.14, bf16[128,768]{1,0:T(8,128)(2,1)} %copy-done.15, bf16[2,128,768]{2,1,0:T(8,128)(2,1)} %copy-done.11, bf16[2,128,768]{2,1,0:T(8,128)(2,1)} %copy-done.12, bf16[128,768]{1,0:T(8,128)(2,1)} %collective-permute-done.3.g, ...), custom_call_target="tpu_custom_call" | custom-call | flops 9437184 | bytes 3145728 | tf_op jit(solution)/shard_map/pallas_call | solution.py:82
  63.7 6.5 %collective-permute-start.13 = (bf16[2,2,192,1152]{3,2,1,0:T(8,128)(2,1)}, bf16[2,2,192,1152]{3,2,1,0:T(8,128)(2,1)S(1)}, u32[]{:S(2)}, u32[]{:S(2)}) collective-permute-start(bf16[2,2,192,1152]{3,2,1,0:T(8,128)(2,1)} %collective-permute-done.12.refs_1_), channel_id=1, source_target_pairs={{0,8},{8,0},{1,9},{9,1},{2,10},{10,2},{3,11},{11,3},{4,12},{12,4},... | collective-permute-start | bytes 5308424 | tf_op jit(solution)/shard_map/ppermute | solution.py:262
  70.2 3.4 %collective-permute-start.14 = (bf16[2,2,192,1152]{3,2,1,0:T(8,128)(2,1)}, bf16[2,2,192,1152]{3,2,1,0:T(8,128)(2,1)}, u32[]{:S(2)}, u32[]{:S(2)}) collective-permute-start(bf16[2,2,192,1152]{3,2,1,0:T(8,128)(2,1)} %collective-permute-done.12.refs_1_), channel_id=1, source_target_pairs={{0,16},{8,120},{16,32},{24,8},{32,48},{40,24},{48,64},{56,40},{64,... | collective-permute-start | bytes 5308424 | tf_op jit(solution)/shard_map/ppermute | solution.py:267
  73.6 0.9 collective-permute-start.6
  74.5 2.5 %collective-permute-start.7 = (bf16[2,384,768]{2,1,0:T(8,128)(2,1)S(1)}, bf16[2,384,768]{2,1,0:T(8,128)(2,1)S(1)}, u32[]{:S(2)}, u32[]{:S(2)}) collective-permute-start(bf16[2,384,768]{2,1,0:T(8,128)(2,1)S(1)} %copy-done.10), channel_id=1, source_target_pairs={{0,3},{1,0},{2,1},{3,2},{4,7},{5,4},{6,5},{7,6},{8,11},{9,8},{10,9... | collective-permute-start | bytes 3538952 | tf_op jit(solution)/shard_map/ppermute | solution.py:259
  77.0 26.4 %collective-permute-done.6.f = bf16[2,384,768]{2,1,0:T(8,128)(2,1)S(1)} collective-permute-done((bf16[2,384,768]{2,1,0:T(8,128)(2,1)S(1)}, bf16[2,384,768]{2,1,0:T(8,128)(2,1)S(1)}, u32[]{:S(2)}, u32[]{:S(2)}) %collective-permute-start.6) | collective-permute-done | bytes 1179680 | tf_op jit(solution)/shard_map/ppermute | solution.py:259
  103.4 0.6 collective-permute-start.15
  104.3 1.1 collective-permute-start.8
  105.5 1.9 collective-permute-start.9
  107.4 13.4 %collective-permute-done.8.g = bf16[384,768]{1,0:T(8,128)(2,1)S(1)} collective-permute-done((bf16[384,768]{1,0:T(8,128)(2,1)S(1)}, bf16[384,768]{1,0:T(8,128)(2,1)S(1)}, u32[]{:S(2)}, u32[]{:S(2)}) %collective-permute-start.8) | collective-permute-done | bytes 589856 | tf_op jit(solution)/shard_map/ppermute | solution.py:259
  120.8 0.8 copy-done.16
  121.6 10.2 %shard_map.56.x_rest = bf16[8,384,768]{2,1,0:T(8,128)(2,1)} custom-call(bf16[384,768]{1,0:T(8,128)(2,1)} %bitcast.23, bf16[384,768]{1,0:T(8,128)(2,1)} %copy-done.7, bf16[2,384,768]{2,1,0:T(8,128)(2,1)} %copy-done.5, bf16[2,384,768]{2,1,0:T(8,128)(2,1)} %copy-done.6, bf16[384,768]{1,0:T(8,128)(2,1)} %copy-done.16, ...), custom_call_target="tpu_custom_call" | custom-call | flops 28311552 | bytes 9437184 | tf_op jit(solution)/shard_map/pallas_call | solution.py:82
  131.9 0.8 collective-permute-start.17
  132.9 9.4 %shard_map.57.refs_0_ = f32[512,1152]{1,0:T(8,128)} custom-call(bf16[8,128,768]{2,1,0:T(8,128)(2,1)} %shard_map.55.x_own, bf16[8,384,768]{2,1,0:T(8,128)(2,1)} %shard_map.56.x_rest, bf16[2,2,192,1152]{3,2,1,0:T(8,128)(2,1)} %copy-done, bf16[2,2,192,1152]{3,2,1,0:T(8,128)(2,1)} %collective-permute-done.12.refs_1_, bf16[2,2,192,1152]{3,2,1,0:T(8,128)(2,1)} %copy-done.8, ...), custom_call_target="tpu_custom_call" | custom-call | flops 4529848320 | bytes 17498112 | tf_op jit(solution)/shard_map/pallas_call | solution.py:160
  142.3 1.2 copy-done.9
  143.5 7.1 %shard_map.58.refs_0_ = f32[512,1152]{1,0:T(8,128)} custom-call(bf16[8,128,768]{2,1,0:T(8,128)(2,1)} %shard_map.55.x_own, bf16[8,384,768]{2,1,0:T(8,128)(2,1)} %shard_map.56.x_rest, f32[512,1152]{1,0:T(8,128)} %shard_map.57.refs_0_, bf16[2,2,192,1152]{3,2,1,0:T(8,128)(2,1)} %copy-done.2, bf16[2,2,192,1152]{3,2,1,0:T(8,128)(2,1)} %copy-done.9), custom_call_target="tpu_custom_call" | custom-call | flops 1811939328 | bytes 9830400 | tf_op jit(solution)/shard_map/pallas_call | solution.py:160
  150.7 1.3 collective-permute-start.19
  152.0 2.1 collective-permute-done.19.refs_2_
  154.1 0.9 copy-done.4
  155.0 4.5 %shard_map.60.refs_0_ = bf16[512,768]{1,0:T(8,128)(2,1)} custom-call(bf16[8,128,768]{2,1,0:T(8,128)(2,1)} %shard_map.55.x_own, bf16[8,384,768]{2,1,0:T(8,128)(2,1)} %shard_map.56.x_rest, f32[512,1152]{1,0:T(8,128)} %shard_map.58.refs_0_, bf16[2,192,1152]{2,1,0:T(8,128)(2,1)} %copy-done.3, bf16[2,192,1152]{2,1,0:T(8,128)(2,1)} %copy-done.4, f32[3,128]{1,0:T(4,128)} %refs_3_.3), custom_call_target="tpu_custom_call" | custom-call | flops 603979776 | bytes 5111808 | tf_op jit(solution)/shard_map/pallas_call | solution.py:160
  160.0 1.2 collective-permute-start.21
  161.2 0.5 collective-permute-start.22
  161.7 4.0 %shard_map.59.q_ref = bf16[512,384]{1,0:T(8,128)(2,1)} custom-call(bf16[8,128,768]{2,1,0:T(8,128)(2,1)} %shard_map.55.x_own, bf16[8,384,768]{2,1,0:T(8,128)(2,1)} %shard_map.56.x_rest, f32[512,1152]{1,0:T(8,128)} %shard_map.58.refs_0_, bf16[2,192,1152]{2,1,0:T(8,128)(2,1)} %copy-done.3, bf16[2,192,1152]{2,1,0:T(8,128)(2,1)} %copy-done.4, f32[3,128]{1,0:T(4,128)} %refs_3_.2), custom_call_target="tpu_custom_call" | custom-call | flops 301989888 | bytes 2949120 | tf_op jit(solution)/shard_map/pallas_call | solution.py:160
  165.7 0.9 copy-done.23
  166.6 7.0 %shard_map.61 = (f32[512,384]{1,0:T(8,128)}, f32[3,512,128]{2,1,0:T(8,128)}) custom-call(bf16[512,384]{1,0:T(8,128)(2,1)} %shard_map.59.q_ref, bf16[512,768]{1,0:T(8,128)(2,1)} %shard_map.60.refs_0_, bf16[512,768]{1,0:T(8,128)(2,1)} %copy-done.23), custom_call_target="tpu_custom_call" | custom-call | flops 1610612736 | bytes 3145728 | tf_op jit(solution)/shard_map/pallas_call | solution.py:244
  173.6 5.6 %collective-permute-done.21.refs_2_ = bf16[512,768]{1,0:T(8,128)(2,1)S(1)} collective-permute-done((bf16[512,768]{1,0:T(8,128)(2,1)}, bf16[512,768]{1,0:T(8,128)(2,1)S(1)}, u32[]{:S(2)}, u32[]{:S(2)}) %collective-permute-start.21) | collective-permute-done | bytes 786464 | tf_op jit(solution)/shard_map/ppermute | solution.py:262
  179.2 0.9 collective-permute-done.22.refs_3_
  180.1 1.3 collective-permute-start.23
  181.4 0.8 collective-permute-start.25
  182.6 0.7 collective-permute-done.23.refs_4_
  183.3 1.1 collective-permute-done.24.refs_5_
  184.4 0.9 copy-done.22
  185.3 11.4 %shard_map.62 = (f32[512,384]{1,0:T(8,128)}, f32[3,512,128]{2,1,0:T(8,128)}) custom-call(bf16[512,384]{1,0:T(8,128)(2,1)} %shard_map.59.q_ref, f32[512,384]{1,0:T(8,128)} %get-tuple-element.29.refs_0_, f32[3,512,128]{2,1,0:T(8,128)} %get-tuple-element.30.refs_1_, bf16[512,768]{1,0:T(8,128)(2,1)} %copy-done.19, bf16[512,768]{1,0:T(8,128)(2,1)} %copy-done.20, ...), custom_call_target="tpu_custom_call" | custom-call | flops 3221225472 | bytes 4718592 | tf_op jit(solution)/shard_map/pallas_call | solution.py:244
  197.3 1.2 collective-permute-done.27.refs_4_
  198.6 0.6 collective-permute-done.28.refs_5_
  199.3 0.6 copy-done.27
  199.9 8.0 %shard_map.63 = bf16[4,128,384]{2,1,0:T(8,128)(2,1)} custom-call(bf16[512,384]{1,0:T(8,128)(2,1)} %shard_map.59.q_ref, f32[512,384]{1,0:T(8,128)} %get-tuple-element.33.refs_0_, f32[3,512,128]{2,1,0:T(8,128)} %get-tuple-element.34.refs_1_, bf16[256,768]{1,0:T(8,128)(2,1)} %copy-done.24, bf16[256,768]{1,0:T(8,128)(2,1)} %copy-done.25, ...), custom_call_target="tpu_custom_call" | custom-call | flops 1610612736 | bytes 3145728 | tf_op jit(solution)/shard_map/pallas_call | solution.py:244
  207.9 17.4 %all_to_all.10 = bf16[4,128,384]{2,1,0:T(8,128)(2,1)S(1)} all-to-all(bf16[4,128,384]{2,1,0:T(8,128)(2,1)} %shard_map.63), channel_id=1, replica_groups=mesh['xl'=2,'zh'=4,'zl'=2,'core'=2,'xh'=2,'y'=4] {'zh'}, dimensions={0} | all-to-all | bytes 786432 | tf_op jit(solution)/shard_map/all_to_all | solution.py:314
  225.6 0.9 copy.12
  (83 shorter events, 4.6 us)
Async XLA Ops:
  0.0 9.1 %copy-start.17 = (bf16[192,3,3,128]{3,0,2,1:T(8,128)(2,1)S(1)}, bf16[192,3,3,128]{3,0,2,1:T(8,128)(2,1)}, u32[]{:S(2)}) copy-start(bf16[192,3,3,128]{3,0,2,1:T(8,128)(2,1)} %param.7) | copy-start | bytes 1327108
  0.0 27.2 %all-to-all-start = ((bf16[4,128,768]{2,1,0:T(8,128)(2,1)}), bf16[4,128,768]{2,1,0:T(8,128)(2,1)S(1)}, u32[]{:S(2)}, u32[]{:S(2)}) async-start(bf16[4,128,768]{2,1,0:T(8,128)(2,1)} %param.5), calls=%async_computation | async-start | bytes 1572864 | tf_op jit(solution)/shard_map/all_to_all | solution.py:273
  9.9 10.8 %collective-permute-start.10 = (bf16[192,1152]{1,0:T(8,128)(2,1)S(1)}, bf16[192,1152]{1,0:T(8,128)(2,1)S(1)}, u32[]{:S(2)}, u32[]{:S(2)}) collective-permute-start(bf16[192,1152]{1,0:T(8,128)(2,1)S(1)} %reshape.14), channel_id=1, source_target_pairs={{0,128},{128,0},{1,129},{129,1},{2,130},{130,2},{3,131},{131,3},{4... | collective-permute-start | bytes 1327112 | tf_op jit(solution)/shard_map/ppermute | solution.py:262
  20.7 0.8 copy-start.18
  27.2 1.2 copy-start.13
  27.5 29.8 %copy-start.1 = (bf16[3,128,768]{2,1,0:T(8,128)(2,1)}, bf16[3,128,768]{2,1,0:T(8,128)(2,1)S(1)}, u32[]{:S(2)}) copy-start(bf16[3,128,768]{2,1,0:T(8,128)(2,1)S(1)} %fusion) | copy-start | bytes 1769476
  28.3 3.8 %collective-permute-start.11 = (bf16[2,192,1152]{2,1,0:T(8,128)(2,1)S(1)}, bf16[2,192,1152]{2,1,0:T(8,128)(2,1)S(1)}, u32[]{:S(2)}, u32[]{:S(2)}) collective-permute-start(bf16[2,192,1152]{2,1,0:T(8,128)(2,1)S(1)} %copy-done.13), channel_id=1, source_target_pairs={{0,8},{8,0},{1,9},{9,1},{2,10},{10,2},{3,11},{11,3},{4,12},{12,4},... | collective-permute-start | bytes 2654216 | tf_op jit(solution)/shard_map/ppermute | solution.py:262
  32.3 26.2 %copy-start = (bf16[2,2,192,1152]{3,2,1,0:T(8,128)(2,1)}, bf16[2,2,192,1152]{3,2,1,0:T(8,128)(2,1)S(1)}, u32[]{:S(2)}) copy-start(bf16[2,2,192,1152]{3,2,1,0:T(8,128)(2,1)S(1)} %pad_maximum_fusion.refs_0_) | copy-start | bytes 5308420
  32.3 31.3 %collective-permute-start.12 = (bf16[2,2,192,1152]{3,2,1,0:T(8,128)(2,1)S(1)}, bf16[2,2,192,1152]{3,2,1,0:T(8,128)(2,1)}, u32[]{:S(2)}, u32[]{:S(2)}) collective-permute-start(bf16[2,2,192,1152]{3,2,1,0:T(8,128)(2,1)S(1)} %pad_maximum_fusion.refs_0_), channel_id=1, source_target_pairs={{0,16},{8,120},{16,32},{24,8},{32,48},{40,24},{48,64},{56,40},{64,... | collective-permute-start | bytes 5308424 | tf_op jit(solution)/shard_map/ppermute | solution.py:267
  35.5 23.0 %copy-start.14 = (bf16[128,768]{1,0:T(8,128)(2,1)}, bf16[128,768]{1,0:T(8,128)(2,1)S(1)}, u32[]{:S(2)}) copy-start(bf16[128,768]{1,0:T(8,128)(2,1)S(1)} %fusion.2.c0) | copy-start | bytes 589828
  35.5 6.1 %collective-permute-start = (bf16[128,768]{1,0:T(8,128)(2,1)S(1)}, bf16[128,768]{1,0:T(8,128)(2,1)S(1)}, u32[]{:S(2)}, u32[]{:S(2)}) collective-permute-start(bf16[128,768]{1,0:T(8,128)(2,1)S(1)} %fusion.2.c0), channel_id=1, source_target_pairs={{0,4},{4,0},{1,5},{5,1},{2,6},{6,2},{3,7},{7,3},{8,12},{12,8},{9,1... | collective-permute-start | bytes 589832 | tf_op jit(solution)/shard_map/ppermute | solution.py:262
  41.6 0.7 copy-start.15
  42.3 8.4 %collective-permute-start.1 = (bf16[2,128,768]{2,1,0:T(8,128)(2,1)S(1)}, bf16[2,128,768]{2,1,0:T(8,128)(2,1)S(1)}, u32[]{:S(2)}, u32[]{:S(2)}) collective-permute-start(bf16[2,128,768]{2,1,0:T(8,128)(2,1)S(1)} %pad_maximum_fusion.3), channel_id=1, source_target_pairs={{0,1},{1,2},{2,3},{3,0},{4,5},{5,6},{6,7},{7,4},{8,9},{9,10},{10,1... | collective-permute-start | bytes 1179656 | tf_op jit(solution)/shard_map/ppermute | solution.py:259
  43.7 7.7 %collective-permute-start.2 = (bf16[2,128,768]{2,1,0:T(8,128)(2,1)S(1)}, bf16[2,128,768]{2,1,0:T(8,128)(2,1)S(1)}, u32[]{:S(2)}, u32[]{:S(2)}) collective-permute-start(bf16[2,128,768]{2,1,0:T(8,128)(2,1)S(1)} %pad_maximum_fusion.3), channel_id=1, source_target_pairs={{0,3},{1,0},{2,1},{3,2},{4,7},{5,4},{6,5},{7,6},{8,11},{9,8},{10,9... | collective-permute-start | bytes 1179656 | tf_op jit(solution)/shard_map/ppermute | solution.py:259
  45.2 12.0 %collective-permute-start.5 = (bf16[384,768]{1,0:T(8,128)(2,1)S(1)}, bf16[384,768]{1,0:T(8,128)(2,1)S(1)}, u32[]{:S(2)}, u32[]{:S(2)}) collective-permute-start(bf16[384,768]{1,0:T(8,128)(2,1)S(1)} %bitcast.21), channel_id=1, source_target_pairs={{0,4},{4,0},{1,5},{5,1},{2,6},{6,2},{3,7},{7,3},{8,12},{12,8},{9,1... | collective-permute-start | bytes 1769480 | tf_op jit(solution)/shard_map/ppermute | solution.py:262
  50.7 7.8 %copy-start.11 = (bf16[2,128,768]{2,1,0:T(8,128)(2,1)}, bf16[2,128,768]{2,1,0:T(8,128)(2,1)S(1)}, u32[]{:S(2)}) copy-start(bf16[2,128,768]{2,1,0:T(8,128)(2,1)S(1)} %collective-permute-done.1.f) | copy-start | bytes 1179652
  51.4 7.0 %collective-permute-start.3 = (bf16[128,768]{1,0:T(8,128)(2,1)}, bf16[128,768]{1,0:T(8,128)(2,1)}, u32[]{:S(2)}, u32[]{:S(2)}) collective-permute-start(bf16[128,768]{1,0:T(8,128)(2,1)} %slice_bitcast_fusion.4), channel_id=1, source_target_pairs={{0,1},{1,2},{2,3},{3,0},{4,5},{5,6},{6,7},{7,4},{8,9},{9,10},{10,1... | collective-permute-start | bytes 589832 | tf_op jit(solution)/shard_map/ppermute | solution.py:259
  51.4 0.7 copy-start.12
  52.9 5.6 %collective-permute-start.4 = (bf16[128,768]{1,0:T(8,128)(2,1)}, bf16[128,768]{1,0:T(8,128)(2,1)}, u32[]{:S(2)}, u32[]{:S(2)}) collective-permute-start(bf16[128,768]{1,0:T(8,128)(2,1)} %slice_bitcast_fusion.3), channel_id=1, source_target_pairs={{0,3},{1,0},{2,1},{3,2},{4,7},{5,4},{6,5},{7,6},{8,11},{9,8},{10,9... | collective-permute-start | bytes 589832 | tf_op jit(solution)/shard_map/ppermute | solution.py:259
  57.2 6.4 %copy-start.7 = (bf16[384,768]{1,0:T(8,128)(2,1)}, bf16[384,768]{1,0:T(8,128)(2,1)S(1)}, u32[]{:S(2)}) copy-start(bf16[384,768]{1,0:T(8,128)(2,1)S(1)} %collective-permute-done.5.c1) | copy-start | bytes 1769476
  58.5 15.1 %copy-start.10 = (bf16[2,384,768]{2,1,0:T(8,128)(2,1)S(1)}, bf16[2,384,768]{2,1,0:T(8,128)(2,1)}, u32[]{:S(2)}) copy-start(bf16[2,384,768]{2,1,0:T(8,128)(2,1)} %pad_maximum_fusion.1) | copy-start | bytes 3538948
  63.7 39.7 %collective-permute-start.13 = (bf16[2,2,192,1152]{3,2,1,0:T(8,128)(2,1)}, bf16[2,2,192,1152]{3,2,1,0:T(8,128)(2,1)S(1)}, u32[]{:S(2)}, u32[]{:S(2)}) collective-permute-start(bf16[2,2,192,1152]{3,2,1,0:T(8,128)(2,1)} %collective-permute-done.12.refs_1_), channel_id=1, source_target_pairs={{0,8},{8,0},{1,9},{9,1},{2,10},{10,2},{3,11},{11,3},{4,12},{12,4},... | collective-permute-start | bytes 5308424 | tf_op jit(solution)/shard_map/ppermute | solution.py:262
  70.2 33.2 %collective-permute-start.14 = (bf16[2,2,192,1152]{3,2,1,0:T(8,128)(2,1)}, bf16[2,2,192,1152]{3,2,1,0:T(8,128)(2,1)}, u32[]{:S(2)}, u32[]{:S(2)}) collective-permute-start(bf16[2,2,192,1152]{3,2,1,0:T(8,128)(2,1)} %collective-permute-done.12.refs_1_), channel_id=1, source_target_pairs={{0,16},{8,120},{16,32},{24,8},{32,48},{40,24},{48,64},{56,40},{64,... | collective-permute-start | bytes 5308424 | tf_op jit(solution)/shard_map/ppermute | solution.py:267
  73.6 29.8 %collective-permute-start.6 = (bf16[2,384,768]{2,1,0:T(8,128)(2,1)S(1)}, bf16[2,384,768]{2,1,0:T(8,128)(2,1)S(1)}, u32[]{:S(2)}, u32[]{:S(2)}) collective-permute-start(bf16[2,384,768]{2,1,0:T(8,128)(2,1)S(1)} %copy-done.10), channel_id=1, source_target_pairs={{0,1},{1,2},{2,3},{3,0},{4,5},{5,6},{6,7},{7,4},{8,9},{9,10},{10,1... | collective-permute-start | bytes 3538952 | tf_op jit(solution)/shard_map/ppermute | solution.py:259
  74.5 28.9 %collective-permute-start.7 = (bf16[2,384,768]{2,1,0:T(8,128)(2,1)S(1)}, bf16[2,384,768]{2,1,0:T(8,128)(2,1)S(1)}, u32[]{:S(2)}, u32[]{:S(2)}) collective-permute-start(bf16[2,384,768]{2,1,0:T(8,128)(2,1)S(1)} %copy-done.10), channel_id=1, source_target_pairs={{0,3},{1,0},{2,1},{3,2},{4,7},{5,4},{6,5},{7,6},{8,11},{9,8},{10,9... | collective-permute-start | bytes 3538952 | tf_op jit(solution)/shard_map/ppermute | solution.py:259
  103.4 18.2 %copy-start.5 = (bf16[2,384,768]{2,1,0:T(8,128)(2,1)}, bf16[2,384,768]{2,1,0:T(8,128)(2,1)S(1)}, u32[]{:S(2)}) copy-start(bf16[2,384,768]{2,1,0:T(8,128)(2,1)S(1)} %collective-permute-done.6.f) | copy-start | bytes 3538948
  103.4 18.2 %copy-start.6 = (bf16[2,384,768]{2,1,0:T(8,128)(2,1)}, bf16[2,384,768]{2,1,0:T(8,128)(2,1)S(1)}, u32[]{:S(2)}) copy-start(bf16[2,384,768]{2,1,0:T(8,128)(2,1)S(1)} %collective-permute-done.7.b) | copy-start | bytes 3538948
  103.4 28.4 %copy-start.8 = (bf16[2,2,192,1152]{3,2,1,0:T(8,128)(2,1)}, bf16[2,2,192,1152]{3,2,1,0:T(8,128)(2,1)S(1)}, u32[]{:S(2)}) copy-start(bf16[2,2,192,1152]{3,2,1,0:T(8,128)(2,1)S(1)} %collective-permute-done.13.refs_2_) | copy-start | bytes 5308420
  103.4 28.4 %collective-permute-start.15 = (bf16[2,2,192,1152]{3,2,1,0:T(8,128)(2,1)}, bf16[2,2,192,1152]{3,2,1,0:T(8,128)(2,1)}, u32[]{:S(2)}, u32[]{:S(2)}) collective-permute-start(bf16[2,2,192,1152]{3,2,1,0:T(8,128)(2,1)} %collective-permute-done.14.refs_3_), channel_id=1, source_target_pairs={{0,8},{8,0},{1,9},{9,1},{2,10},{10,2},{3,11},{11,3},{4,12},{12,4},... | collective-permute-start | bytes 5308424 | tf_op jit(solution)/shard_map/ppermute | solution.py:262
  104.0 27.9 %collective-permute-start.16 = (bf16[2,2,192,1152]{3,2,1,0:T(8,128)(2,1)}, bf16[2,2,192,1152]{3,2,1,0:T(8,128)(2,1)S(1)}, u32[]{:S(2)}, u32[]{:S(2)}) collective-permute-start(bf16[2,2,192,1152]{3,2,1,0:T(8,128)(2,1)} %collective-permute-done.14.refs_3_), channel_id=1, source_target_pairs={{0,16},{8,120},{16,32},{24,8},{32,48},{40,24},{48,64},{56,40},{64,... | collective-permute-start | bytes 5308424 | tf_op jit(solution)/shard_map/ppermute | solution.py:267
  104.3 16.4 %collective-permute-start.8 = (bf16[384,768]{1,0:T(8,128)(2,1)S(1)}, bf16[384,768]{1,0:T(8,128)(2,1)S(1)}, u32[]{:S(2)}, u32[]{:S(2)}) collective-permute-start(bf16[384,768]{1,0:T(8,128)(2,1)S(1)} %slice_bitcast_fusion.2), channel_id=1, source_target_pairs={{0,1},{1,2},{2,3},{3,0},{4,5},{5,6},{6,7},{7,4},{8,9},{9,10},{10,1... | collective-permute-start | bytes 1769480 | tf_op jit(solution)/shard_map/ppermute | solution.py:259
  105.5 16.1 %collective-permute-start.9 = (bf16[384,768]{1,0:T(8,128)(2,1)S(1)}, bf16[384,768]{1,0:T(8,128)(2,1)}, u32[]{:S(2)}, u32[]{:S(2)}) collective-permute-start(bf16[384,768]{1,0:T(8,128)(2,1)S(1)} %slice_bitcast_fusion.1), channel_id=1, source_target_pairs={{0,3},{1,0},{2,1},{3,2},{4,7},{5,4},{6,5},{7,6},{8,11},{9,8},{10,9... | collective-permute-start | bytes 1769480 | tf_op jit(solution)/shard_map/ppermute | solution.py:259
  120.8 0.8 copy-start.16
  131.9 10.4 %copy-start.2 = (bf16[2,2,192,1152]{3,2,1,0:T(8,128)(2,1)}, bf16[2,2,192,1152]{3,2,1,0:T(8,128)(2,1)S(1)}, u32[]{:S(2)}) copy-start(bf16[2,2,192,1152]{3,2,1,0:T(8,128)(2,1)S(1)} %collective-permute-done.16.refs_1_) | copy-start | bytes 5308420
  131.9 10.4 %collective-permute-start.17 = (bf16[2,2,192,1152]{3,2,1,0:T(8,128)(2,1)S(1)}, bf16[2,2,192,1152]{3,2,1,0:T(8,128)(2,1)S(1)}, u32[]{:S(2)}, u32[]{:S(2)}) collective-permute-start(bf16[2,2,192,1152]{3,2,1,0:T(8,128)(2,1)S(1)} %collective-permute-done.16.refs_1_), channel_id=1, source_target_pairs={{0,8},{8,0},{1,9},{9,1},{2,10},{10,2},{3,11},{11,3},{4,12},{12,4},... | collective-permute-start | bytes 5308424 | tf_op jit(solution)/shard_map/ppermute | solution.py:262
  132.8 17.9 %collective-permute-start.18 = (bf16[2,192,1152]{2,1,0:T(8,128)(2,1)S(1)}, bf16[2,192,1152]{2,1,0:T(8,128)(2,1)S(1)}, u32[]{:S(2)}, u32[]{:S(2)}) collective-permute-start(bf16[2,192,1152]{2,1,0:T(8,128)(2,1)S(1)} %slice_bitcast_fusion), channel_id=1, source_target_pairs={{0,16},{8,120},{16,32},{24,8},{32,48},{40,24},{48,64},{56,40},{64,... | collective-permute-start | bytes 2654216 | tf_op jit(solution)/shard_map/ppermute | solution.py:267
  142.3 1.2 copy-start.9
  150.7 3.4 %copy-start.3 = (bf16[2,192,1152]{2,1,0:T(8,128)(2,1)}, bf16[2,192,1152]{2,1,0:T(8,128)(2,1)S(1)}, u32[]{:S(2)}) copy-start(bf16[2,192,1152]{2,1,0:T(8,128)(2,1)S(1)} %collective-permute-done.18.refs_1_) | copy-start | bytes 2654212
  150.7 3.4 %collective-permute-start.19 = (bf16[2,192,1152]{2,1,0:T(8,128)(2,1)S(1)}, bf16[2,192,1152]{2,1,0:T(8,128)(2,1)S(1)}, u32[]{:S(2)}, u32[]{:S(2)}) collective-permute-start(bf16[2,192,1152]{2,1,0:T(8,128)(2,1)S(1)} %collective-permute-done.18.refs_1_), channel_id=1, source_target_pairs={{0,8},{8,0},{1,9},{9,1},{2,10},{10,2},{3,11},{11,3},{4,12},{12,4},... | collective-permute-start | bytes 2654216 | tf_op jit(solution)/shard_map/ppermute | solution.py:262
  154.1 0.9 copy-start.4
  159.5 6.1 %collective-permute-start.20 = (bf16[512,768]{1,0:T(8,128)(2,1)}, bf16[512,768]{1,0:T(8,128)(2,1)S(1)}, u32[]{:S(2)}, u32[]{:S(2)}) collective-permute-start(bf16[512,768]{1,0:T(8,128)(2,1)} %shard_map.60.refs_0_), channel_id=1, source_target_pairs={{0,8},{8,0},{1,9},{9,1},{2,10},{10,2},{3,11},{11,3},{4,12},{12,4},... | collective-permute-start | bytes 2359304 | tf_op jit(solution)/shard_map/ppermute | solution.py:262
  160.0 19.2 %collective-permute-start.21 = (bf16[512,768]{1,0:T(8,128)(2,1)}, bf16[512,768]{1,0:T(8,128)(2,1)S(1)}, u32[]{:S(2)}, u32[]{:S(2)}) collective-permute-start(bf16[512,768]{1,0:T(8,128)(2,1)} %shard_map.60.refs_0_), channel_id=1, source_target_pairs={{0,128},{128,0},{1,129},{129,1},{2,130},{130,2},{3,131},{131,3},{4... | collective-permute-start | bytes 2359304 | tf_op jit(solution)/shard_map/ppermute | solution.py:262
  161.2 18.9 %collective-permute-start.22 = (bf16[512,768]{1,0:T(8,128)(2,1)}, bf16[512,768]{1,0:T(8,128)(2,1)S(1)}, u32[]{:S(2)}, u32[]{:S(2)}) collective-permute-start(bf16[512,768]{1,0:T(8,128)(2,1)} %shard_map.60.refs_0_), channel_id=1, source_target_pairs={{0,16},{16,0},{1,17},{17,1},{2,18},{18,2},{3,19},{19,3},{4,20},{20... | collective-permute-start | bytes 2359304 | tf_op jit(solution)/shard_map/ppermute | solution.py:262
  165.7 0.9 copy-start.23
  179.2 5.2 %copy-start.19 = (bf16[512,768]{1,0:T(8,128)(2,1)}, bf16[512,768]{1,0:T(8,128)(2,1)S(1)}, u32[]{:S(2)}) copy-start(bf16[512,768]{1,0:T(8,128)(2,1)S(1)} %collective-permute-done.21.refs_2_) | copy-start | bytes 2359300
  180.1 4.3 %copy-start.20 = (bf16[512,768]{1,0:T(8,128)(2,1)}, bf16[512,768]{1,0:T(8,128)(2,1)S(1)}, u32[]{:S(2)}) copy-start(bf16[512,768]{1,0:T(8,128)(2,1)S(1)} %collective-permute-done.22.refs_3_) | copy-start | bytes 2359300
  180.1 3.2 %collective-permute-start.23 = (bf16[512,768]{1,0:T(8,128)(2,1)S(1)}, bf16[512,768]{1,0:T(8,128)(2,1)S(1)}, u32[]{:S(2)}, u32[]{:S(2)}) collective-permute-start(bf16[512,768]{1,0:T(8,128)(2,1)S(1)} %collective-permute-done.21.refs_2_), channel_id=1, source_target_pairs={{0,8},{8,0},{1,9},{9,1},{2,10},{10,2},{3,11},{11,3},{4,12},{12,4},... | collective-permute-start | bytes 2359304 | tf_op jit(solution)/shard_map/ppermute | solution.py:262
  181.4 3.0 %collective-permute-start.24 = (bf16[512,768]{1,0:T(8,128)(2,1)S(1)}, bf16[512,768]{1,0:T(8,128)(2,1)S(1)}, u32[]{:S(2)}, u32[]{:S(2)}) collective-permute-start(bf16[512,768]{1,0:T(8,128)(2,1)S(1)} %collective-permute-done.22.refs_3_), channel_id=1, source_target_pairs={{0,8},{8,0},{1,9},{9,1},{2,10},{10,2},{3,11},{11,3},{4,12},{12,4},... | collective-permute-start | bytes 2359304 | tf_op jit(solution)/shard_map/ppermute | solution.py:262
  181.4 15.3 %collective-permute-start.25 = (bf16[256,768]{1,0:T(8,128)(2,1)S(1)}, bf16[256,768]{1,0:T(8,128)(2,1)S(1)}, u32[]{:S(2)}, u32[]{:S(2)}) collective-permute-start(bf16[256,768]{1,0:T(8,128)(2,1)S(1)} %slice.30), channel_id=1, source_target_pairs={{0,16},{16,0},{1,17},{17,1},{2,18},{18,2},{3,19},{19,3},{4,20},{20... | collective-permute-start | bytes 1179656 | tf_op jit(solution)/shard_map/ppermute | solution.py:262
  182.2 14.5 %collective-permute-start.26 = (bf16[256,768]{1,0:T(8,128)(2,1)S(1)}, bf16[256,768]{1,0:T(8,128)(2,1)S(1)}, u32[]{:S(2)}, u32[]{:S(2)}) collective-permute-start(bf16[256,768]{1,0:T(8,128)(2,1)S(1)} %slice.31), channel_id=1, source_target_pairs={{0,128},{128,0},{1,129},{129,1},{2,130},{130,2},{3,131},{131,3},{4... | collective-permute-start | bytes 1179656 | tf_op jit(solution)/shard_map/ppermute | solution.py:262
  183.3 1.1 copy-start.21
  184.4 0.9 copy-start.22
  196.7 2.4 %copy-start.24 = (bf16[256,768]{1,0:T(8,128)(2,1)}, bf16[256,768]{1,0:T(8,128)(2,1)S(1)}, u32[]{:S(2)}) copy-start(bf16[256,768]{1,0:T(8,128)(2,1)S(1)} %collective-permute-done.25.refs_2_) | copy-start | bytes 1179652
  196.7 2.4 %copy-start.25 = (bf16[256,768]{1,0:T(8,128)(2,1)}, bf16[256,768]{1,0:T(8,128)(2,1)S(1)}, u32[]{:S(2)}) copy-start(bf16[256,768]{1,0:T(8,128)(2,1)S(1)} %collective-permute-done.26.refs_3_) | copy-start | bytes 1179652
  196.7 1.8 collective-permute-start.27
  197.2 1.9 collective-permute-start.28
  198.6 0.8 copy-start.26
  199.1 0.8 copy-start.27
